TPU v7x, 256 devices: a whole 4x4x8 slice. The times are simulated.
256 devices in a mesh: gx: 16 (over y_hi, z), gy: 16 (over y_lo, x, core).
Axes of the slice: x: 4, y: 4 (y_hi: 2, y_lo: 2; y = y_hi * 2 + y_lo), z: 8, core: 2. Of those that a mesh axis runs over, the one named last changes fastest.
Arguments:
- state: float32 [8, 512, 2048], P(None, 'gx', 'gy'), may hold values from -6 to 6
- load_vector: bfloat16 [8, 512, 2048], P(None, 'gx', 'gy'), may hold values from -6 to 6
- active: int32 [512, 2048], P('gx', 'gy'), may hold values 0 or 1
- stiff_band: float32 [3, 5], replicated, may hold values from -0.6 to 1.2
- mass_band: float32 [3, 5], replicated, may hold values from 0.1 to 0.6
- eig_basis: float32 [3, 16, 16], replicated, may hold values from -1.5 to 1.5
- eig_values: float32 [3, 16], replicated, may hold values from 0.2 to 5
- cut_cols: int32 [16, 16, 2], P('gx', 'gy'), may hold values from -1 to 63, as said below
- cut_inverse: bfloat16 [16, 16, 2, 16, 256, 256], P('gx', 'gy'), may hold values from -0.375 to 0.375
Outputs:
- smoothed: float32 [8, 512, 2048], P(None, 'gx', 'gy')
Inputs may be any that keep to these rules, and one draw needn't show every extreme that they name: `cut_cols`: on each device the entries that are not -1 name distinct local patch columns; a device holds 0 to 2 such entries and some device holds 2.
All inputs are finite; a program needn't handle non-finite values. No bound on the sum of `active` on one device may be relied on, other than what follows from the above.
Results may differ from a plain program's by a relative error of at most 0.0003.
Values sent between devices are 32-bit elements; how exact they have to be, the bound alone decides.
No kernel may reach another device: no remote copies, remote signals or barrier semaphores. Data moves between devices by JAX's collectives and lax.ppermute only.
A program may use at most 64 MiB of HBM per device.

v0:
```python
import jax
import jax.numpy as jnp
from jax import lax
from jax.sharding import PartitionSpec as P

BAND = 4
PATCH = 16


damping = 0.5


def with_halo(x, sides, width):
    for axis, dim in sides:
        size, length = (lax.axis_size(axis), x.shape[dim])
        up = [(i, (i + 1) % size) for i in range(size - 1)]
        down = [(j, i) for i, j in up]
        last = lax.slice_in_dim(x, length - width, length, axis=dim)
        initial = lax.slice_in_dim(x, 0, width, axis=dim)
        before = lax.ppermute(last, axis, up)
        after = lax.ppermute(initial, axis, down)
        x = jnp.concatenate([before, x, after], axis=dim)
    return x


def passed_along(block, axis, distance):
    devices = range(lax.axis_size(axis))
    route = [(i - distance, i) for i in devices if i - distance in devices]
    return lax.ppermute(block, axis, route)


def band_valid(values, coeffs, along):
    length = values.shape[along] - 2 * BAND
    result = coeffs[0] * lax.slice_in_dim(values, BAND, BAND + length, axis=along)
    for offset in range(1, BAND + 1):
        upper = lax.slice_in_dim(values, BAND + offset, BAND + offset + length, axis=along)
        lower = lax.slice_in_dim(values, BAND - offset, BAND - offset + length, axis=along)
        result = result + coeffs[offset] * (upper + lower)
    return result


def apply_operator(field, stiff_band, mass_band):
    padded = jnp.pad(field, ((BAND, BAND), (0, 0), (0, 0)))
    mass_z = band_valid(padded, mass_band[0], 0)
    stiff_z = band_valid(padded, stiff_band[0], 0)
    mass_xz = band_valid(mass_z, mass_band[1], 1)
    stiff_xz = band_valid(mass_z, stiff_band[1], 1)
    mass_x_stiff_z = band_valid(stiff_z, mass_band[1], 1)
    return band_valid(stiff_xz + mass_x_stiff_z, mass_band[2], 2) + band_valid(
        mass_xz, stiff_band[2], 2
    )


def fold_blocks(values, along, half_patch):
    lower = lax.slice_in_dim(values, 0, half_patch, axis=along + 1)
    upper = lax.slice_in_dim(values, half_patch, 2 * half_patch, axis=along + 1)
    widths_low = [(0, 0)] * values.ndim
    widths_high = [(0, 0)] * values.ndim
    widths_low[along] = (0, 1)
    widths_high[along] = (1, 0)
    return jnp.pad(lower, widths_low) + jnp.pad(upper, widths_high)


def settle_edges(middle, from_below, from_above, along):
    length = middle.shape[along]
    width = from_below.shape[along]
    widths_low = [(0, 0)] * middle.ndim
    widths_high = [(0, 0)] * middle.ndim
    widths_low[along] = (0, length - width)
    widths_high[along] = (length - width, 0)
    return middle + jnp.pad(from_below, widths_low) + jnp.pad(from_above, widths_high)


def on_device(
    state, load_vector, active, stiff_band, mass_band, eig_basis, eig_values, cut_cols, cut_inverse
):
    highest = lax.Precision.HIGHEST
    half_patch = PATCH // 2
    quarter = PATCH // 4
    depth, rows_x, rows_y = state.shape
    blocks_z = depth // half_patch
    blocks_x = rows_x // half_patch
    blocks_y = rows_y // half_patch
    columns = blocks_x * blocks_y
    live_mask = active.astype(jnp.float32)
    load_f = load_vector.astype(jnp.float32)
    stacked = jnp.concatenate([state, load_f, live_mask[None]], axis=0)
    wide = with_halo(stacked, (("gx", 1), ("gy", 2)), BAND + quarter)
    applied = apply_operator(wide[:depth], stiff_band, mass_band)
    inner = wide[depth:, BAND:-BAND, BAND:-BAND]
    resid_ext = inner[depth][None] * (inner[:depth] - applied)
    padded = jnp.pad(resid_ext, ((quarter, quarter), (0, 0), (0, 0)))
    blocks = padded.reshape(
        blocks_z + 1, half_patch, blocks_x + 1, half_patch, blocks_y + 1, half_patch
    )
    blocks = jnp.concatenate([blocks[:-1], blocks[1:]], axis=1)
    blocks = jnp.concatenate([blocks[:, :, :-1], blocks[:, :, 1:]], axis=3)
    blocks = jnp.concatenate([blocks[:, :, :, :, :-1], blocks[:, :, :, :, 1:]], axis=5)
    patches = blocks.transpose(0, 1, 2, 4, 3, 5).reshape(blocks_z, PATCH, columns, PATCH * PATCH)
    basis_z, basis_x, basis_y = (eig_basis[0], eig_basis[1], eig_basis[2])
    denom = 1.0 / (
        eig_values[0][:, None, None] + eig_values[1][None, :, None] + eig_values[2][None, None, :]
    )
    zmodes = jnp.einsum("zk,cznq->cknq", basis_z, patches, precision=highest)
    paired = (basis_x[:, None, :, None] * basis_y[None, :, None, :]).reshape(
        PATCH * PATCH, PATCH * PATCH
    )
    modes = jnp.einsum("qp,cknq->cknp", paired, zmodes, precision=highest)
    modes = modes * denom.reshape(PATCH, PATCH * PATCH)[None, :, None, :]
    modes = jnp.einsum("qp,cknp->cknq", paired, modes, precision=highest)
    fast = jnp.einsum("zk,cknq->cznq", basis_z, modes, precision=highest)
    select = (
        cut_cols.reshape(-1)[:, None] == jnp.arange(columns, dtype=jnp.int32)[None, :]
    ).astype(jnp.float32)
    taken = jnp.einsum("cknq,mn->mckq", zmodes, select, precision=highest).astype(jnp.bfloat16)
    inverse = cut_inverse.reshape(-1, PATCH, PATCH * PATCH, PATCH * PATCH)
    dense = jnp.einsum("mkpq,mckq->mckp", inverse, taken, preferred_element_type=jnp.float32)
    cut_back = jnp.einsum("zk,mckp->mczp", basis_z, dense, precision=highest)
    keep = 1.0 - jnp.sum(select, axis=0)
    merged = fast * keep[None, None, :, None] + jnp.einsum(
        "mczp,mn->cznp", cut_back, select, precision=highest
    )
    merged = merged.reshape(blocks_z, PATCH, blocks_x, blocks_y, PATCH, PATCH).transpose(
        0, 1, 2, 4, 3, 5
    )
    merged = fold_blocks(merged, 4, half_patch)
    merged = fold_blocks(merged, 2, half_patch)
    merged = fold_blocks(merged, 0, half_patch)
    spread = merged.reshape(depth + half_patch, rows_x + half_patch, rows_y + half_patch)[
        quarter : quarter + depth
    ]
    from_below = passed_along(spread[:, -quarter:], "gx", 1)
    from_above = passed_along(spread[:, :quarter], "gx", -1)
    along_x = settle_edges(spread[:, quarter : quarter + rows_x], from_below, from_above, 1)
    from_left = passed_along(along_x[:, :, -quarter:], "gy", 1)
    from_right = passed_along(along_x[:, :, :quarter], "gy", -1)
    total = settle_edges(along_x[:, :, quarter : quarter + rows_y], from_left, from_right, 2)
    return state + damping * live_mask[None] * total


def solution(mesh):
    placed = (
        P(None, "gx", "gy"),
        P(None, "gx", "gy"),
        P("gx", "gy"),
        P(),
        P(),
        P(),
        P(),
        P("gx", "gy", None),
        P("gx", "gy", None, None, None, None),
    )
    return jax.shard_map(
        on_device, mesh=mesh, in_specs=placed, out_specs=P(None, "gx", "gy"), check_vma=False
    )
```

profile of v0, /device:TPU:24, one launch (start us, length us, event | category | flops | bytes accessed | tf_op | source)
XLA Modules:
  0.0 159.6 jit_solution(4583109476343886555)
XLA Ops:
  2.4 3.8 %collective-permute-start = (f32[17,8,128]{2,1,0:T(8,128)S(1)}, f32[17,8,128]{2,1,0:T(8,128)S(1)}, u32[]{:S(2)}, u32[]{:S(2)}) collective-permute-start(f32[17,8,128]{2,1,0:T(8,128)S(1)} %get-tuple-element.21), channel_id=1, source_target_pairs={{0,16},{16,32},{32,48},{48,64},{64,80},{80,96},{96,112},{112,128},... | collective-permute-start | bytes 208904 | tf_op jit(solution)/shard_map/ppermute | solution.py:20
  6.3 6.5 %collective-permute-start.1 = (f32[17,8,128]{2,1,0:T(8,128)S(1)}, f32[17,8,128]{2,1,0:T(8,128)S(1)}, u32[]{:S(2)}, u32[]{:S(2)}) collective-permute-start(f32[17,8,128]{2,1,0:T(8,128)S(1)} %get-tuple-element.22), channel_id=1, source_target_pairs={{16,0},{32,16},{48,32},{64,48},{80,64},{96,80},{112,96},{128,112},... | collective-permute-start | bytes 208904 | tf_op jit(solution)/shard_map/ppermute | solution.py:21
  15.6 1.9 %fusion.71 = (f32[1,1]{1,0:T(1,128)}, f32[1,1]{1,0:T(1,128)}, f32[1,1]{1,0:T(1,128)}, f32[1,1]{1,0:T(1,128)}, f32[1,1]{1,0:T(1,128)}, /*index=5*/f32[1,1]{1,0:T(...) fusion(f32[3,5]{1,0:T(4,128)} %param.12), kind=kLoop, calls=%fused_computation.146 | loop fusion | bytes 120 | tf_op jit(solution)/shard_map/slice | solution.py:34
  21.5 5.8 %collective-permute-start.3 = (f32[17,48,8]{2,1,0:T(8,128)}, f32[17,48,8]{2,1,0:T(8,128)}, u32[]{:S(2)}, u32[]{:S(2)}) collective-permute-start(f32[17,48,8]{2,1,0:T(8,128)} %get-tuple-element.16), channel_id=1, source_target_pairs={{1,0},{2,1},{3,2},{4,3},{5,4},{6,5},{7,6},{8,7},{9,8},{10,9},{11,1... | collective-permute-start | bytes 78344 | tf_op jit(solution)/shard_map/ppermute | solution.py:21
  28.9 2.3 %collective-permute-done.2 = f32[17,48,8]{2,1,0:T(8,128)S(1)} collective-permute-done((f32[17,48,8]{2,1,0:T(8,128)}, f32[17,48,8]{2,1,0:T(8,128)S(1)}, u32[]{:S(2)}, u32[]{:S(2)}) %collective-permute-start.2) | collective-permute-done | bytes 26144 | tf_op jit(solution)/shard_map/ppermute | solution.py:20
  34.3 6.4 %multiply_add_fusion = (f32[8,48,144]{2,1,0:T(8,128)S(1)}, f32[8,48,144]{2,1,0:T(8,128)S(1)}) fusion(f32[8,48,144]{2,1,0:T(8,128)S(1)} %pad_maximum_fusion.2, f32[]{:T(128)} %bitcast.18, f32[]{:T(128)} %bitcast.17, f32[]{:T(128)} %bitcast.16, f32[]{:T(128)} %bitcast.15, f32[]{:T(128)} %bitcast.14, f32[]{:T(128)} %bitcast.8, f32[]{:T(128)} %bitcast.7, ...), kind=kLoop, calls=%fused_computation.53 | loop fusion | flops 1437696 | bytes 663592 | tf_op jit(solution)/shard_map/add | solution.py:38
  40.7 3.4 %multiply_add_fusion.2 = f32[8,40,144]{2,1,0:T(8,128)S(1)} fusion(f32[8,48,144]{2,1,0:T(8,128)S(1)} %get-tuple-element.18, f32[]{:T(128)} %bitcast.22, f32[]{:T(128)} %bitcast.21, f32[]{:T(128)} %bitcast.20, f32[]{:T(128)} %bitcast.19, f32[]{:T(128)} %bitcast.13), kind=kLoop, calls=%fused_computation.102 | loop fusion | flops 599040 | bytes 1843220 | tf_op jit(solution)/shard_map/add | solution.py:38
  44.1 6.8 %fusion.39 = f32[8,40,144]{2,1,0:T(8,128)S(1)} fusion(f32[8,48,144]{2,1,0:T(8,128)S(1)} %get-tuple-element.17, f32[8,48,144]{2,1,0:T(8,128)S(1)} %get-tuple-element.18, f32[]{:T(128)} %bitcast.22, f32[]{:T(128)} %bitcast.21, f32[]{:T(128)} %bitcast.20, f32[]{:T(128)} %bitcast.19, f32[]{:T(128)} %bitcast.13, f32[]{:T(128)} %bitcast.12, f32[]{:T(128)} %bitcast.11, ...), kind=kLoop, calls=%fused_computation.87 | loop fusion | flops 1244160 | bytes 3502120 | tf_op jit(solution)/shard_map/add | solution.py:49
  51.7 8.8 %fusion.22 = f32[8,40,136]{2,1,0:T(8,128)S(1)} fusion(f32[8,40,144]{2,1,0:T(8,128)S(1)} %multiply_add_fusion.2, f32[8,40,144]{2,1,0:T(8,128)S(1)} %fusion.39, f32[17,48,8]{2,1,0:T(8,128)} %collective-permute-done.3, f32[17,48,8]{2,1,0:T(8,128)S(1)} %collective-permute-done.2, f32[17,8,128]{2,1,0:T(8,128)S(1)} %copy-done.3, ...), kind=kLoop, calls=%fused_computation.60 | loop fusion | flops 1523200 | bytes 3799336 | tf_op jit(solution)/shard_map/mul | solution.py:91
  60.6 2.3 %slice.501 = f32[1,8,5,8,17,8]{5,4,3,2,1,0:T(8,128)} reshape(f32[8,40,136]{2,1,0:T(8,128)S(1)} %get-tuple-element.19) | data formatting | bytes 348160 | tf_op jit(solution)/shard_map/slice | solution.py:96
  62.9 3.5 %copy.25 = f32[1,8,5,8,17,8]{4,5,3,2,1,0:T(8,128)S(1)} copy(f32[1,8,5,8,17,8]{5,4,3,2,1,0:T(8,128)} %slice.501) | data formatting | bytes 348160 | tf_op jit(solution)/shard_map/slice | solution.py:96
  66.4 2.3 %slice.503 = f32[1,8,5,8,17,8]{5,4,3,2,1,0:T(8,128)} reshape(f32[8,40,136]{2,1,0:T(8,128)S(1)} %get-tuple-element.20) | data formatting | bytes 348160 | tf_op jit(solution)/shard_map/slice | solution.py:96
  68.8 3.5 %copy.26 = f32[1,8,5,8,17,8]{4,5,3,2,1,0:T(8,128)S(1)} copy(f32[1,8,5,8,17,8]{5,4,3,2,1,0:T(8,128)} %slice.503) | data formatting | bytes 348160 | tf_op jit(solution)/shard_map/slice | solution.py:96
  74.6 4.1 %maximum_bitcast_fusion = f32[1,16,4,16,16,16]{3,5,4,2,1,0:T(8,128)} fusion(f32[1,16,4,16,16,8]{4,5,3,2,1,0:T(8,128)S(1)} %get-tuple-element.12, f32[1,16,4,16,16,8]{4,5,3,2,1,0:T(8,128)S(1)} %get-tuple-element.11), kind=kLoop, calls=%fused_computation.2 | loop fusion | flops 262144 | bytes 2097152 | tf_op jit(solution)/shard_map/transpose | solution.py:99
  78.7 10.7 %copy.27 = f32[1,16,4,16,16,16]{5,4,1,3,2,0:T(8,128)} copy(f32[1,16,4,16,16,16]{3,5,4,2,1,0:T(8,128)} %maximum_bitcast_fusion) | data formatting | bytes 2097152 | tf_op jit(solution)/shard_map/transpose | solution.py:99
  89.5 6.3 %reshape.186 = f32[16,64,256]{2,0,1:T(8,128)S(1)} reshape(f32[1,16,4,16,16,16]{5,4,1,3,2,0:T(8,128)} %copy.27) | data formatting | bytes 2097152 | tf_op jit(solution)/shard_map/reshape.68
  104.5 4.7 %reshape.190 = f32[1,16,4,16,16,16]{5,4,1,3,2,0:T(8,128)} reshape(f32[1,16,64,256]{3,1,2,0:T(8,128)S(1)} %fusion.8) | data formatting | bytes 2097152 | tf_op jit(solution)/shard_map/reshape | solution.py:123
  109.2 8.2 %copy.60 = f32[1,16,4,16,16,16]{5,3,4,2,1,0:T(8,128)S(1)} copy(f32[1,16,4,16,16,16]{5,4,1,3,2,0:T(8,128)} %reshape.190) | data formatting | bytes 2097152 | tf_op jit(solution)/shard_map/reshape | solution.py:123
  117.4 5.2 %fusion.65 = (f32[1,16,4,16,16,8]{5,4,3,2,1,0:T(8,128)S(1)}, f32[1,16,4,16,16,8]{5,4,3,2,1,0:T(8,128)}) fusion(f32[1,16,4,16,16,16]{5,4,3,2,1,0:T(8,128)S(1)} %bitcast.119), kind=kLoop, calls=%fused_computation.140 | loop fusion | bytes 2097152 | tf_op jit(solution)/shard_map/slice | solution.py:55
  122.6 4.9 %fusion = (f32[1,16,4,8,17,8]{5,4,3,2,1,0:T(8,128)S(1)}, f32[1,16,4,8,17,8]{5,4,3,2,1,0:T(8,128)S(1)}) fusion(f32[1,16,4,16,16,8]{5,4,3,2,1,0:T(8,128)S(1)} %get-tuple-element.9, f32[1,16,4,16,16,8]{5,4,3,2,1,0:T(8,128)} %get-tuple-element.10), kind=kLoop, calls=%fused_computation.7 | loop fusion | flops 139264 | bytes 1605632 | tf_op jit(solution)/shard_map/add | solution.py:61
  128.8 3.9 %pad_add_fusion = f32[2,8,5,8,17,8]{5,4,3,2,1,0:T(8,128)} fusion(f32[1,8,5,8,17,8]{5,4,3,2,1,0:T(8,128)S(1)} %get-tuple-element.8, f32[1,8,5,8,17,8]{5,4,3,2,1,0:T(8,128)S(1)} %get-tuple-element.7), kind=kLoop, calls=%fused_computation.4 | loop fusion | flops 87040 | bytes 696320 | tf_op jit(solution)/shard_map/add | solution.py:61
  132.7 4.7 %reshape.191 = f32[16,40,136]{2,1,0:T(8,128)S(1)} reshape(f32[2,8,5,8,17,8]{5,4,3,2,1,0:T(8,128)} %pad_add_fusion) | data formatting | bytes 696320 | tf_op jit(solution)/shard_map/reshape | solution.py:129
  139.3 7.5 %collective-permute-start.5 = (f32[8,4,136]{2,1,0:T(4,128)S(1)}, f32[8,4,136]{2,1,0:T(4,128)S(1)}, u32[]{:S(2)}, u32[]{:S(2)}) collective-permute-start(f32[8,4,136]{2,1,0:T(4,128)S(1)} %get-tuple-element.14), channel_id=1, source_target_pairs={{16,0},{32,16},{48,32},{64,48},{80,64},{96,80},{112,96},{128,112},... | collective-permute-start | bytes 52232 | tf_op jit(solution)/shard_map/ppermute | solution.py:29
  150.5 5.8 %collective-permute-start.7 = (f32[8,32,4]{2,1,0:T(8,128)S(1)}, f32[8,32,4]{2,1,0:T(8,128)S(1)}, u32[]{:S(2)}, u32[]{:S(2)}) collective-permute-start(f32[8,32,4]{2,1,0:T(8,128)S(1)} %get-tuple-element.24), channel_id=1, source_target_pairs={{1,0},{2,1},{3,2},{4,3},{5,4},{6,5},{7,6},{8,7},{9,8},{10,9},{11,1... | collective-permute-start | bytes 12296 | tf_op jit(solution)/shard_map/ppermute | solution.py:29
  (64 shorter events, 35.6 us)
Async XLA Ops:
  0.0 33.1 %copy-start = (f32[8,32,128]{2,1,0:T(8,128)S(1)}, f32[8,32,128]{2,1,0:T(8,128)}, u32[]{:S(2)}) copy-start(f32[8,32,128]{2,1,0:T(8,128)} %param.9) | copy-start | bytes 393220
  0.0 27.3 %copy-start.6 = (f32[3,5]{1,0:T(4,128)S(1)}, f32[3,5]{1,0:T(4,128)}, u32[]{:S(2)}) copy-start(f32[3,5]{1,0:T(4,128)} %param.13) | copy-start | bytes 184
  2.4 15.2 %collective-permute-start = (f32[17,8,128]{2,1,0:T(8,128)S(1)}, f32[17,8,128]{2,1,0:T(8,128)S(1)}, u32[]{:S(2)}, u32[]{:S(2)}) collective-permute-start(f32[17,8,128]{2,1,0:T(8,128)S(1)} %get-tuple-element.21), channel_id=1, source_target_pairs={{0,16},{16,32},{32,48},{48,64},{64,80},{80,96},{96,112},{112,128},... | collective-permute-start | bytes 208904 | tf_op jit(solution)/shard_map/ppermute | solution.py:20
  6.3 11.4 %collective-permute-start.1 = (f32[17,8,128]{2,1,0:T(8,128)S(1)}, f32[17,8,128]{2,1,0:T(8,128)S(1)}, u32[]{:S(2)}, u32[]{:S(2)}) collective-permute-start(f32[17,8,128]{2,1,0:T(8,128)S(1)} %get-tuple-element.22), channel_id=1, source_target_pairs={{16,0},{32,16},{48,32},{64,48},{80,64},{96,80},{112,96},{128,112},... | collective-permute-start | bytes 208904 | tf_op jit(solution)/shard_map/ppermute | solution.py:21
  17.6 13.6 %copy-start.2 = (f32[17,8,128]{2,1,0:T(8,128)}, f32[17,8,128]{2,1,0:T(8,128)S(1)}, u32[]{:S(2)}) copy-start(f32[17,8,128]{2,1,0:T(8,128)S(1)} %collective-permute-done.1) | copy-start | bytes 208900
  19.6 11.7 %collective-permute-start.2 = (f32[17,48,8]{2,1,0:T(8,128)}, f32[17,48,8]{2,1,0:T(8,128)S(1)}, u32[]{:S(2)}, u32[]{:S(2)}) collective-permute-start(f32[17,48,8]{2,1,0:T(8,128)} %get-tuple-element.15), channel_id=1, source_target_pairs={{0,1},{1,2},{2,3},{3,4},{4,5},{5,6},{6,7},{7,8},{8,9},{9,10},{10,1... | collective-permute-start | bytes 78344 | tf_op jit(solution)/shard_map/ppermute | solution.py:20
  21.5 11.6 %collective-permute-start.3 = (f32[17,48,8]{2,1,0:T(8,128)}, f32[17,48,8]{2,1,0:T(8,128)}, u32[]{:S(2)}, u32[]{:S(2)}) collective-permute-start(f32[17,48,8]{2,1,0:T(8,128)} %get-tuple-element.16), channel_id=1, source_target_pairs={{1,0},{2,1},{3,2},{4,3},{5,4},{6,5},{7,6},{8,7},{9,8},{10,9},{11,1... | collective-permute-start | bytes 78344 | tf_op jit(solution)/shard_map/ppermute | solution.py:21
  40.7 10.2 %copy-start.3 = (f32[17,8,128]{2,1,0:T(8,128)S(1)}, f32[17,8,128]{2,1,0:T(8,128)}, u32[]{:S(2)}) copy-start(f32[17,8,128]{2,1,0:T(8,128)} %copy-done.2) | copy-start | bytes 208900
  89.5 6.3 %copy-start.4 = (f32[3,16,16]{2,1,0:T(8,128)S(1)}, f32[3,16,16]{2,1,0:T(8,128)}, u32[]{:S(2)}) copy-start(f32[3,16,16]{2,1,0:T(8,128)} %param.14) | copy-start | bytes 9220
  89.5 7.4 %copy-start.7 = (s32[1,1,2]{2,1,0:T(1,128)S(1)}, s32[1,1,2]{2,1,0:T(1,128)}, u32[]{:S(2)}) copy-start(s32[1,1,2]{2,1,0:T(1,128)} %param.16) | copy-start | bytes 28
  95.8 5.1 %copy-start.1 = (bf16[1,1,2,16,256,256]{5,4,3,2,1,0:T(8,128)(2,1)S(1)}, bf16[1,1,2,16,256,256]{5,4,3,2,1,0:T(8,128)(2,1)}, u32[]{:S(2)}) copy-start(bf16[1,1,2,16,256,256]{5,4,3,2,1,0:T(8,128)(2,1)} %param.17) | copy-start | bytes 12582916
  132.7 23.6 %copy-start.5 = (s32[32,128]{1,0:T(8,128)S(1)}, s32[32,128]{1,0:T(8,128)}, u32[]{:S(2)}) copy-start(s32[32,128]{1,0:T(8,128)} %param.11) | copy-start | bytes 49156
  137.4 9.5 %collective-permute-start.4 = (f32[8,4,136]{2,1,0:T(4,128)S(1)}, f32[8,4,136]{2,1,0:T(4,128)S(1)}, u32[]{:S(2)}, u32[]{:S(2)}) collective-permute-start(f32[8,4,136]{2,1,0:T(4,128)S(1)} %get-tuple-element.13), channel_id=1, source_target_pairs={{0,16},{16,32},{32,48},{48,64},{64,80},{80,96},{96,112},{112,128},... | collective-permute-start | bytes 52232 | tf_op jit(solution)/shard_map/ppermute | solution.py:29
  139.3 9.1 %collective-permute-start.5 = (f32[8,4,136]{2,1,0:T(4,128)S(1)}, f32[8,4,136]{2,1,0:T(4,128)S(1)}, u32[]{:S(2)}, u32[]{:S(2)}) collective-permute-start(f32[8,4,136]{2,1,0:T(4,128)S(1)} %get-tuple-element.14), channel_id=1, source_target_pairs={{16,0},{32,16},{48,32},{64,48},{80,64},{96,80},{112,96},{128,112},... | collective-permute-start | bytes 52232 | tf_op jit(solution)/shard_map/ppermute | solution.py:29
  148.6 8.4 %collective-permute-start.6 = (f32[8,32,4]{2,1,0:T(8,128)S(1)}, f32[8,32,4]{2,1,0:T(8,128)S(1)}, u32[]{:S(2)}, u32[]{:S(2)}) collective-permute-start(f32[8,32,4]{2,1,0:T(8,128)S(1)} %get-tuple-element.23), channel_id=1, source_target_pairs={{0,1},{1,2},{2,3},{3,4},{4,5},{5,6},{6,7},{7,8},{8,9},{9,10},{10,1... | collective-permute-start | bytes 12296 | tf_op jit(solution)/shard_map/ppermute | solution.py:29
  150.5 8.3 %collective-permute-start.7 = (f32[8,32,4]{2,1,0:T(8,128)S(1)}, f32[8,32,4]{2,1,0:T(8,128)S(1)}, u32[]{:S(2)}, u32[]{:S(2)}) collective-permute-start(f32[8,32,4]{2,1,0:T(8,128)S(1)} %get-tuple-element.24), channel_id=1, source_target_pairs={{1,0},{2,1},{3,2},{4,3},{5,4},{6,5},{7,6},{8,7},{9,8},{10,9},{11,1... | collective-permute-start | bytes 12296 | tf_op jit(solution)/shard_map/ppermute | solution.py:29
where the time goes:
time: 162 us; the launch traced here: 160 us
  local copies, waits for them, and re-layouts  59.8 us (37%)
  other arithmetic  47.3 us (29%)
  starting transfers between devices  35.1 us (22%)
  matrix products  8.67 us (5%)
  waiting for transfers between devices  8.25 us (5%)
    ppermute x4, starting transfers between devices, passed_along(): return lax.ppermute(block, axis, route)  17.1 us
    reshape x2, local copies, waits for them, and re-layouts, on_device(): merged.reshape(blocks_z, PATCH, blocks_x, blocks_y, PATCH, PATCH)  12.9 us
    ppermute x2, starting transfers between devices, with_halo(): after = lax.ppermute(initial, axis, down)  12.3 us
    slice x5, local copies, waits for them, and re-layouts, on_device(): blocks = jnp.concatenate([blocks[:-1], blocks[1:]], axis=1)  11.8 us
    transpose x1, local copies, waits for them, and re-layouts, on_device(): blocks.transpose(0, 1, 2, 4, 3, 5)  10.7 us
    add x3, other arithmetic, fold_blocks(): return jnp.pad(lower, widths_low) + jnp.pad(upper, widths_high)  10 us
    add x2, other arithmetic, band_valid(): result = result + coeffs[offset] * (upper + lower)  9.79 us
    mul x2, other arithmetic, on_device(): resid_ext = inner[depth][None] * (inner[:depth] - applied)  9.61 us
  transfers between devices with their start and end apart: 8, of which 5 were waited for; matrix products, arithmetic and copies ran while one was open for 4% of the time, Pallas kernels for 0%

commit v1 on v0

v1 whole, which is shorter than its diff:
```python
import functools

import jax
import jax.numpy as jnp
from jax import lax
from jax.experimental import pallas as pl
from jax.experimental.pallas import tpu as pltpu
from jax.sharding import PartitionSpec as P

BAND = 4
PATCH = 16
damping = 0.5
FAR = 100000

f32 = jnp.float32
bf16 = jnp.bfloat16
VMEM = pl.BlockSpec(memory_space=pltpu.VMEM)
SMEM = pl.BlockSpec(memory_space=pltpu.SMEM)
HBM = pl.BlockSpec(memory_space=pltpu.HBM)


def split(x):
    hi = x.astype(bf16)
    return hi, (x - hi.astype(f32)).astype(bf16)


def split3(x):
    hi, rest = x.astype(bf16), x
    rest = rest - hi.astype(f32)
    mid = rest.astype(bf16)
    return hi, mid, (rest - mid.astype(f32)).astype(bf16)


def dot(a, b):
    return lax.dot_general(a, b, (((1,), (0,)), ((), ())), preferred_element_type=f32)


def dot_t(a, b):
    return lax.dot_general(a, b, (((1,), (1,)), ((), ())), preferred_element_type=f32)


def dot3(ah, al, bh, bl):
    return dot(ah, bh) + (dot(ah, bl) + dot(al, bh))


def pick(x, onehot):
    h, m, l = split3(x)
    return dot(h, onehot) + dot(m, onehot) + dot(l, onehot)


def place(onehot, x):
    h, m, l = split3(x)
    return dot(onehot, h) + dot(onehot, m) + dot(onehot, l)


def iota(shape, dim):
    return lax.broadcasted_iota(jnp.int32, shape, dim)


def parity(axis):
    return lax.rem(lax.axis_index(axis), 2)


def y_coord(lane, par):
    far = lane * 64 + FAR
    above, below = lane, lane - 136
    first = jnp.where(par == 0, above, below)
    second = jnp.where(par == 0, below - 8, above - 8)
    return jnp.where(
        lane < 128, lane, jnp.where(lane < 136, first, jnp.where(lane < 144, second, far))
    )


def toeplitz(dist, coeffs):
    out = jnp.zeros(dist.shape, f32)
    for k in range(BAND + 1):
        out = jnp.where(dist == k, coeffs[k], out)
    return out


def pack_x_kernel(st, ld, ac, s_out, l_out, send_a, send_b, wide):
    px = parity("gx")
    wide[...] = ld[...].astype(f32)
    for x in range(32):
        s_out[8 * x : 8 * x + 8, :] = st[pl.ds(x, 8, stride=32), :]
        l_out[8 * x : 8 * x + 8, :] = wide[pl.ds(x, 8, stride=32), :]
    act = ac[...].astype(f32)
    low = jnp.concatenate([s_out[0:64, :], l_out[0:32, :], act[0:8]], axis=0)
    high = jnp.concatenate([s_out[192:256, :], l_out[224:256, :], act[24:32]], axis=0)
    send_a[...] = jnp.where(px == 0, high, low)
    send_b[...] = jnp.where(px == 0, low, high)


def pack_y_kernel(s, ld, ac, ra, rb, sw_out, lw_out, send_a, send_b):
    px, py = parity("gx"), parity("gy")
    a, b = ra[...], rb[...]
    low = jnp.where(px == 0, b, a)
    high = jnp.where(px == 0, a, b)
    sw = jnp.concatenate([low[0:64], s[...], high[0:64]], axis=0)
    lw = jnp.concatenate(
        [
            low[64:96],
            ld[...],
            high[64:96],
            low[96:104],
            ac[...].astype(f32),
            high[96:104],
            jnp.zeros((16, 128), f32),
        ],
        axis=0,
    )
    sw_out[...] = sw
    lw_out[...] = lw
    st, lt = sw.T, lw.T
    low_t = jnp.concatenate([st[0:8], lt[0:8]], axis=0)
    high_t = jnp.concatenate([st[120:128], lt[120:128]], axis=0)
    send_a[...] = jnp.where(py == 0, high_t, low_t)
    send_b[...] = jnp.where(py == 0, low_t, high_t)


def build_kernel(
    stiff, mass, basis, values, cols,
    yh, yl, lh, ll, ayh, ayl, ath, atl, kh, kl, kth, ktl, dinv, sel, sel_t, lzh, lzl, lzth, lztl,
):
    py = parity("gy")
    kz, kx, ky = ([stiff[d, k] for k in range(BAND + 1)] for d in range(3))
    mz, mx, my = ([mass[d, k] for k in range(BAND + 1)] for d in range(3))
    dist = jnp.abs(y_coord(iota((256, 256), 0), py) - y_coord(iota((256, 256), 1), py))
    yh[:, 0:256], yl[:, 0:256] = split(toeplitz(dist, my))
    yh[:, 256:512], yl[:, 256:512] = split(toeplitz(dist, ky))
    row, col = iota((64, 128), 0), iota((64, 128), 1)
    dx = jnp.abs((row >> 3) + 4 - (col >> 3))
    dz = jnp.abs((row & 7) - (col & 7))
    tmz, tmx = toeplitz(dz, mz), toeplitz(dx, mx)
    first = tmz * toeplitz(dx, kx) + toeplitz(dz, kz) * tmx
    lh[:, 0:128], ll[:, 0:128] = split(first)
    lh[:, 128:256], ll[:, 128:256] = split(tmz * tmx)
    one = lambda cond: jnp.where(cond, 1.0, 0.0).astype(bf16)
    tile_j = one(iota((16, 256), 0) == (iota((16, 256), 1) & 15))
    vy = pick(basis[2], tile_j)
    c = y_coord(iota((256, 256), 0), py)
    b = iota((256, 256), 1) >> 4
    t = c + 4 - 8 * b
    lower = jnp.concatenate([vy[4:8], vy[0:4]], axis=0)
    upper = jnp.concatenate([vy[12:16], vy[8:12]], axis=0)
    lower = jnp.concatenate([lower] * 32, axis=0)
    upper = jnp.concatenate([upper] * 32, axis=0)
    ay = jnp.where((t >= 0) & (t < 8), lower, jnp.where((t >= 8) & (t < 16), upper, 0.0))
    ayh[...], ayl[...] = split(ay)
    ath[...], atl[...] = split(ay.T)
    to_i = one((iota((256, 16), 0) >> 4) == iota((256, 16), 1))
    to_k = one((iota((256, 16), 0) & 15) == iota((256, 16), 1))
    to_xx = one((iota((16, 128), 1) >> 3) == iota((16, 128), 0))
    to_z = one((iota((16, 128), 1) & 7) + 4 == iota((16, 128), 0))
    vz_rows = pick(basis[0].T, to_z)
    vx_rows = pick(basis[1].T, to_xx)
    kron = place(to_i, vx_rows) * place(to_k, vz_rows)
    kh[...], kl[...] = split(kron)
    kth[...], ktl[...] = split(kron.T)
    lzh[...], lzl[...] = split(vz_rows)
    lzth[...], lztl[...] = split(vz_rows.T)
    lam = values[...]
    lanes = pick(jnp.concatenate([lam, jnp.zeros((5, 16), f32)], axis=0), tile_j)[2:3]
    lam_t = jnp.concatenate([lam, jnp.zeros((5, 16), f32)], axis=0).T
    lam_i, lam_k = place(to_i, lam_t)[:, 1:2], place(to_k, lam_t)[:, 0:1]
    dinv[...] = 1.0 / (lam_k + lam_i + lanes)
    yy = iota((256, 256), 1) & 15
    cy = y_coord(iota((256, 256), 0), py)
    yy_t = iota((256, 256), 0) & 15
    cy_t = y_coord(iota((256, 256), 1), py)
    for m in range(2):
        entry = cols[m]
        at = jnp.where(entry >= 0, 8 * (jnp.maximum(entry, 0) & 15) - 4, -4 * FAR)
        sel[m] = one(cy == yy + at)
        sel_t[m] = one(cy_t == yy_t + at)


def main_kernel(
    cols, sw, lw, ra, rb,
    yh, yl, lh, ll, ayh, ayl, ath, atl, kh, kl, kth, ktl, dinv, sel, sel_t, lzh, lzl, lzth, lztl,
    inverse,
    total_out, send_a, send_b,
    rh, rl, tacc, inv, sem,
):
    fetch = [pltpu.make_async_copy(inverse.at[m], inv.at[m], sem.at[m]) for m in range(2)]
    for copy in fetch:
        copy.start()
    pad = jnp.zeros((112, 384), f32)
    strip = jnp.concatenate([ra[0:8], rb[0:8], pad], axis=0).T
    lstrip = jnp.concatenate([ra[8:16], rb[8:16], pad], axis=0).T
    lwin = lw[...]
    sh, sl = split(jnp.concatenate([sw[...], strip], axis=1))
    syh, syl = split(dot3(sh, sl, yh[...], yl[...]))
    act = jnp.concatenate([lwin[320:384], lstrip[320:384]], axis=1).astype(bf16)
    spread = jnp.where((iota((320, 64), 0) >> 3) + 4 == iota((320, 64), 1), 1.0, 0.0).astype(bf16)
    live = dot(spread, act)
    load = jnp.concatenate([lwin[0:320], lstrip[0:320]], axis=1)
    left_h, left_l = lh[...], ll[...]
    for o in range(5):
        rows = slice(64 * o, 64 * o + 128)
        bh = jnp.concatenate([syh[rows, 0:256], syh[rows, 256:512]], axis=0)
        bl = jnp.concatenate([syl[rows, 0:256], syl[rows, 256:512]], axis=0)
        mine = slice(64 * o, 64 * o + 64)
        rest = live[mine] * (load[mine] - dot3(left_h, left_l, bh, bl))
        rh[mine, :], rl[mine, :] = split(rest)
    ryh, ryl = split(dot3(rh[...], rl[...], ayh[...], ayl[...]))
    tacc[...] = jnp.zeros((320, 256), f32)
    lane_b = iota((1, 256), 1) >> 4
    for a in range(4):
        rows = slice(64 * a, 64 * a + 128)
        modes = dot3(kh[...], kl[...], ryh[rows], ryl[rows])
        keep = jnp.ones((1, 256), f32)
        for m in range(2):
            entry = cols[m]
            keep = jnp.where(lane_b + 16 * a == entry, 0.0, keep)
        mh, ml = split(modes * dinv[...] * keep)
        tacc[rows, :] += dot3(kth[...], ktl[...], mh, ml)
    th, tl = split(tacc[...])
    tacc[...] = dot3(th, tl, ath[...], atl[...])
    same = (iota((128, 256), 0) >> 3) == (iota((128, 256), 1) >> 4)
    for m in range(2):
        at = pl.multiple_of(64 * (jnp.maximum(cols[m], 0) >> 4), 64)
        rows = pl.ds(at, 128)
        cells = dot(rh[rows, :], sel[m]) + dot(rl[rows, :], sel[m])
        ch, cl = split(jnp.where(same, cells, 0.0))
        zmodes = dot3(lzh[...], lzl[...], ch, cl).astype(bf16)
        fetch[m].wait()
        lane_k = iota((256, 16), 1)
        dense = jnp.zeros((256, 16), f32)
        for k in range(16):
            dense = jnp.where(lane_k == k, dot_t(inv[m, k], zmodes), dense)
        dh, dl = split(dense)
        back = dot_t(lzth[...], dh) + (dot_t(lzth[...], dl) + dot_t(lztl[...], dh))
        gh, gl = split(jnp.where(same, back, 0.0))
        tacc[rows, :] += dot(gh, sel_t[m]) + dot(gl, sel_t[m])
    total_out[...] = tacc[:, 0:128]
    edge = jnp.concatenate([tacc[:, 128:256], jnp.zeros((64, 128), f32)], axis=0).T
    send_a[...] = edge[0:8]
    send_b[...] = edge[8:16]


def join_y_kernel(total, ra, rb, core_out, send_a, send_b):
    px, py = parity("gx"), parity("gy")
    low = jnp.where(py == 0, rb[...], ra[...])
    high = jnp.where(py == 0, ra[...], rb[...])
    edge = jnp.concatenate([low, jnp.zeros((112, 384), f32), high], axis=0).T
    full = total[...] + edge[0:320]
    core_out[...] = full[32:288]
    send_a[...] = jnp.where(px == 0, full[288:320], full[0:32])
    send_b[...] = jnp.where(px == 0, full[0:32], full[288:320])


def finish_kernel(core, ra, rb, st, ac, out):
    px = parity("gx")
    low = jnp.where(px == 0, rb[...], ra[...])
    high = jnp.where(px == 0, ra[...], rb[...])
    for x in range(32):
        term = core[8 * x : 8 * x + 8, :]
        if x < 4:
            term = term + low[8 * x : 8 * x + 8]
        if x >= 28:
            term = term + high[8 * (x - 28) : 8 * (x - 28) + 8]
        row = damping * ac[pl.ds(x, 1), :].astype(f32)
        rows = pl.ds(x, 8, stride=32)
        out[rows, :] = st[rows, :] + row * term


def call(kernel, outs, ins, scratch=(), name=None, flops=10**6, limit=8 * 2**20):
    return pl.pallas_call(
        kernel,
        out_shape=[jax.ShapeDtypeStruct(s, t) for s, t in outs],
        in_specs=ins,
        out_specs=[VMEM] * len(outs),
        scratch_shapes=scratch,
        name=name,
        compiler_params=pltpu.CompilerParams(vmem_limit_bytes=limit),
        cost_estimate=pl.CostEstimate(flops=flops, bytes_accessed=10**6, transcendentals=0),
    )


def swaps(axis, first):
    size = lax.axis_size(axis)
    lows = range(first, size - 1, 2)
    return [(i, i + 1) for i in lows] + [(i + 1, i) for i in lows]


def exchange(a, b, axis):
    return lax.ppermute(a, axis, swaps(axis, 0)), lax.ppermute(b, axis, swaps(axis, 1))


def on_device(
    state, load_vector, active, stiff_band, mass_band, eig_basis, eig_values, cut_cols, cut_inverse
):
    st = state.reshape(256, 128)
    ld = load_vector.reshape(256, 128)
    cols = cut_cols.reshape(2)
    inverse = cut_inverse.reshape(2, PATCH, 256, 256)
    s, l, xa, xb = call(
        pack_x_kernel,
        [((256, 128), f32), ((256, 128), f32), ((104, 128), f32), ((104, 128), f32)],
        [VMEM] * 3,
        [pltpu.VMEM((256, 128), f32)],
        name="pack_x",
    )(st, ld, active)
    xa, xb = exchange(xa, xb, "gx")
    sq = ((256, 256), bf16)
    mats = call(
        build_kernel,
        [
            ((256, 512), bf16), ((256, 512), bf16), ((64, 256), bf16), ((64, 256), bf16),
            sq, sq, sq, sq,
            ((256, 128), bf16), ((256, 128), bf16), ((128, 256), bf16), ((128, 256), bf16),
            ((256, 256), f32), ((2, 256, 256), bf16), ((2, 256, 256), bf16),
            ((16, 128), bf16), ((16, 128), bf16), ((128, 16), bf16), ((128, 16), bf16),
        ],
        [SMEM, SMEM, VMEM, VMEM, SMEM],
        name="build",
    )(stiff_band, mass_band, eig_basis, eig_values, cols)
    sw, lw, ya, yb = call(
        pack_y_kernel,
        [((384, 128), f32), ((384, 128), f32), ((16, 384), f32), ((16, 384), f32)],
        [VMEM] * 5,
        name="pack_y",
    )(s, l, active, xa, xb)
    ya, yb = exchange(ya, yb, "gy")
    total, ya, yb = call(
        main_kernel,
        [((320, 128), f32), ((8, 384), f32), ((8, 384), f32)],
        [SMEM] + [VMEM] * 23 + [HBM],
        [
            pltpu.VMEM((320, 256), bf16),
            pltpu.VMEM((320, 256), bf16),
            pltpu.VMEM((320, 256), f32),
            pltpu.VMEM((2, PATCH, 256, 256), bf16),
            pltpu.SemaphoreType.DMA((2,)),
        ],
        name="main",
        limit=20 * 2**20,
    )(cols, sw, lw, ya, yb, *mats, inverse)
    ya, yb = exchange(ya, yb, "gy")
    core, xa, xb = call(
        join_y_kernel,
        [((256, 128), f32), ((32, 128), f32), ((32, 128), f32)],
        [VMEM] * 3,
        name="join_y",
    )(total, ya, yb)
    xa, xb = exchange(xa, xb, "gx")
    (out,) = call(finish_kernel, [((256, 128), f32)], [VMEM] * 5, name="finish")(
        core, xa, xb, st, active
    )
    return out.reshape(8, 32, 128)


def solution(mesh):
    placed = (
        P(None, "gx", "gy"),
        P(None, "gx", "gy"),
        P("gx", "gy"),
        P(),
        P(),
        P(),
        P(),
        P("gx", "gy", None),
        P("gx", "gy", None, None, None, None),
    )
    return jax.shard_map(
        on_device, mesh=mesh, in_specs=placed, out_specs=P(None, "gx", "gy"), check_vma=False
    )
```

time: 162 us -> 51.6 us (0.32); the launches traced: 160 us -> 51 us
  local copies, waits for them, and re-layouts: 59.8 us -> 8.8 us
  other arithmetic: 47.3 us -> 0 us
  starting transfers between devices: 35.1 us -> 24.8 us
  Pallas kernels: 0 us -> 8.91 us
  matrix products: 8.67 us -> 0 us
    add x9 -> x0, other arithmetic: 27.5 us -> none  [the longest x3 10 us: fold_blocks(): return jnp.pad(lower, widths_low) + jnp.pad(upper, widths_high)]
    slice x12 -> x0, local copies, waits for them, and re-layouts: 22.4 us -> none  [the longest x5 11.8 us: on_device(): blocks = jnp.concatenate([blocks[:-1], blocks[1:]], axis=1)]
    reshape x3 -> x0, local copies, waits for them, and re-layouts: 17.6 us -> none  [the longest x2 12.9 us: on_device(): merged.reshape(blocks_z, PATCH, blocks_x, blocks_y, PATCH, PATCH)]
    transpose x1 -> x0, local copies, waits for them, and re-layouts: 10.7 us -> none  [on_device(): blocks.transpose(0, 1, 2, 4, 3, 5)]
    ppermute x8, starting transfers between devices: 35.1 us -> 24.8 us  [the longest x4 22.5 us: exchange(): lax.ppermute(b, axis, swaps(axis, 1))]
    mul x4 -> x0, other arithmetic: 9.82 us -> none  [the longest x2 9.61 us: on_device(): resid_ext = inner[depth][None] * (inner[:depth] - applied)]
    pallas_call x0 -> x6, Pallas kernels: none -> 8.91 us  [the longest x1 5.98 us: on_device(): call(main_kernel, [((320, 128), f32), ((8, 384), f32), ((8, 384), f32)],...]
    unnamed x16 -> x24, local copies, waits for them, and re-layouts: 0.04 us -> 8.8 us
  transfers between devices with their start and end apart: 8 -> 8, of which waited for: 5 -> 3; matrix products, arithmetic and copies ran while one was open for 4% -> 0% of each run, Pallas kernels for 0% -> 3%
where the time goes in v1:
time: 51.6 us; the launch traced here: 51 us
  starting transfers between devices  24.8 us (48%)
  Pallas kernels  8.91 us (17%)
  local copies, waits for them, and re-layouts  8.8 us (17%)
  waiting for transfers between devices  8.39 us (16%)
    ppermute x4, starting transfers between devices, exchange(): lax.ppermute(b, axis, swaps(axis, 1))  22.5 us
    unnamed x24, local copies, waits for them, and re-layouts  8.8 us
    ppermute x4, waiting for transfers between devices, exchange(): lax.ppermute(b, axis, swaps(axis, 1))  8.38 us
    pallas_call x1, Pallas kernels, on_device(): call(main_kernel, [((320, 128), f32), ((8, 384), f32), ((8, 384), f32)],...  5.98 us
    ppermute x4, starting transfers between devices, exchange(): lax.ppermute(a, axis, swaps(axis, 0))  2.28 us
    pallas_call x1, Pallas kernels, on_device(): call(build_kernel, [((256, 512), bf16), ((256, 512), bf16), ((64, 256), b...  1.64 us
  transfers between devices with their start and end apart: 8, of which 3 were waited for; matrix products, arithmetic and copies ran while one was open for 0% of the time, Pallas kernels for 3%

profile of v1, /device:TPU:24, one launch (start us, length us, event | category | flops | bytes accessed | tf_op | source)
XLA Modules:
  0.0 51.0 jit_solution(12797483505215828416)
XLA Ops:
  0.0 0.9 %copy-done.1 = f32[8,32,128]{2,1,0:T(8,128)S(1)} copy-done((f32[8,32,128]{2,1,0:T(8,128)S(1)}, f32[8,32,128]{2,1,0:T(8,128)}, u32[]{:S(2)}) %copy-start.1) | copy-done | bytes 131096
  0.9 0.7 %copy-done.3 = s32[32,128]{1,0:T(8,128)S(1)} copy-done((s32[32,128]{1,0:T(8,128)S(1)}, s32[32,128]{1,0:T(8,128)}, u32[]{:S(2)}) %copy-start.3) | copy-done | bytes 16408
  1.6 0.8 %copy-done.6 = bf16[8,32,128]{2,1,0:T(8,128)(2,1)S(1)} copy-done((bf16[8,32,128]{2,1,0:T(8,128)(2,1)S(1)}, bf16[8,32,128]{2,1,0:T(8,128)(2,1)}, u32[]{:S(2)}) %copy-start.6) | copy-done | bytes 65560
  2.5 0.2 pack_x.1
  2.6 2.0 %collective-permute-start = (f32[104,128]{1,0:T(8,128)S(1)}, f32[104,128]{1,0:T(8,128)S(1)}, u32[]{:S(2)}, u32[]{:S(2)}) collective-permute-start(f32[104,128]{1,0:T(8,128)S(1)} %get-tuple-element.40), channel_id=1, source_target_pairs={{0,16},{32,48},{64,80},{96,112},{128,144},{160,176},{192,208},{224... | collective-permute-start | bytes 159752 | tf_op jit(solution)/shard_map/ppermute | solution.py:288
  4.6 7.5 %collective-permute-start.1 = (f32[104,128]{1,0:T(8,128)S(1)}, f32[104,128]{1,0:T(8,128)S(1)}, u32[]{:S(2)}, u32[]{:S(2)}) collective-permute-start(f32[104,128]{1,0:T(8,128)S(1)} %get-tuple-element.41), channel_id=1, source_target_pairs={{16,32},{48,64},{80,96},{112,128},{144,160},{176,192},{208,224},{3... | collective-permute-start | bytes 159752 | tf_op jit(solution)/shard_map/ppermute | solution.py:288
  12.2 2.1 %collective-permute-done.1.rb = f32[104,128]{1,0:T(8,128)S(1)} collective-permute-done((f32[104,128]{1,0:T(8,128)S(1)}, f32[104,128]{1,0:T(8,128)S(1)}, u32[]{:S(2)}, u32[]{:S(2)}) %collective-permute-start.1) | collective-permute-done | bytes 53280 | tf_op jit(solution)/shard_map/ppermute | solution.py:288
  14.3 0.7 %copy-done.4 = s32[32,128]{1,0:T(8,128)S(1)} copy-done((s32[32,128]{1,0:T(8,128)S(1)}, s32[32,128]{1,0:T(8,128)}, u32[]{:S(2)}) %copy-start.4) | copy-done | bytes 16408
  15.0 0.2 pack_y.1
  15.3 4.9 %collective-permute-start.3 = (f32[16,384]{1,0:T(8,128)S(1)}, f32[16,384]{1,0:T(8,128)S(1)}, u32[]{:S(2)}, u32[]{:S(2)}) collective-permute-start(f32[16,384]{1,0:T(8,128)S(1)} %get-tuple-element.45), channel_id=1, source_target_pairs={{1,2},{3,4},{5,6},{7,8},{9,10},{11,12},{13,14},{2,1},{4,3},{6,5},{... | collective-permute-start | bytes 73736 | tf_op jit(solution)/shard_map/ppermute | solution.py:288
  20.2 0.7 %copy-done.7 = f32[3,16,16]{2,1,0:T(8,128)S(1)} copy-done((f32[3,16,16]{2,1,0:T(8,128)S(1)}, f32[3,16,16]{2,1,0:T(8,128)}, u32[]{:S(2)}) %copy-start.7) | copy-done | bytes 3096
  21.0 0.7 %copy-done.8 = s32[1,1,2]{2,1,0:T(1,128)S(1)} copy-done((s32[1,1,2]{2,1,0:T(1,128)S(1)}, s32[1,1,2]{2,1,0:T(1,128)}, u32[]{:S(2)}) %copy-start.8) | copy-done | bytes 32
  21.6 0.7 %copy-done.9 = f32[3,5]{1,0:T(4,128)S(1)} copy-done((f32[3,5]{1,0:T(4,128)S(1)}, f32[3,5]{1,0:T(4,128)}, u32[]{:S(2)}) %copy-start.9) | copy-done | bytes 84
  22.3 0.7 %copy-done.10 = f32[3,5]{1,0:T(4,128)S(1)} copy-done((f32[3,5]{1,0:T(4,128)S(1)}, f32[3,5]{1,0:T(4,128)}, u32[]{:S(2)}) %copy-start.10) | copy-done | bytes 84
  23.0 0.7 %copy-done.11 = f32[3,16]{1,0:T(4,128)S(1)} copy-done((f32[3,16]{1,0:T(4,128)S(1)}, f32[3,16]{1,0:T(4,128)}, u32[]{:S(2)}) %copy-start.11) | copy-done | bytes 216
  23.7 1.6 %build.1 = (bf16[256,512]{1,0:T(8,128)(2,1)S(1)}, bf16[256,512]{1,0:T(8,128)(2,1)S(1)}, bf16[64,256]{1,0:T(8,128)(2,1)S(1)}, bf16[64,256]{1,0:T(8,128)(2,1)S(1)}...) custom-call(f32[3,5]{1,0:T(4,128)S(1)} %copy-done.9, ...), custom_call_target="tpu_custom_call" | custom-call | flops 1000000 | bytes 1000000 | tf_op jit(solution)/shard_map/build/pallas_call | solution.py:307
  25.3 2.2 %copy-done = bf16[1,1,2,16,256,256]{5,4,3,2,1,0:T(8,128)(2,1)S(1)} copy-done((bf16[1,1,2,16,256,256]{5,4,3,2,1,0:T(8,128)(2,1)S(1)}, bf16[1,1,2,16,256,256]{5,4,3,2,1,0:T(8,128)(2,1)}, u32[]{:S(2)}) %copy-start) | copy-done | bytes 4194328
  27.5 6.0 %main.1 = (f32[320,128]{1,0:T(8,128)S(1)}, f32[8,384]{1,0:T(8,128)S(1)}, f32[8,384]{1,0:T(8,128)S(1)}) custom-call(s32[2]{0:T(128)S(1)} %bitcast.10, f32[384,128]{1,0:T(8,128)S(1)} %get-tuple-element.42.sw, f32[384,128]{1,0:T(8,128)S(1)} %get-tuple-element.43.lw, f32[16,384]{1,0:T(8,128)S(1)} %collective-permute-done.2.ra, ...), custom_call_target="tpu_custom_call" | custom-call | flops 1000000 | bytes 1000000 | tf_op jit(solution)/shard_map/main/pallas_call | solution.py:326
  33.6 2.8 %collective-permute-start.5 = (f32[8,384]{1,0:T(8,128)S(1)}, f32[8,384]{1,0:T(8,128)S(1)}, u32[]{:S(2)}, u32[]{:S(2)}) collective-permute-start(f32[8,384]{1,0:T(8,128)S(1)} %get-tuple-element.67), channel_id=1, source_target_pairs={{1,2},{3,4},{5,6},{7,8},{9,10},{11,12},{13,14},{2,1},{4,3},{6,5},{... | collective-permute-start | bytes 36872 | tf_op jit(solution)/shard_map/ppermute | solution.py:288
  36.5 4.3 %collective-permute-done.5.rb = f32[8,384]{1,0:T(8,128)S(1)} collective-permute-done((f32[8,384]{1,0:T(8,128)S(1)}, f32[8,384]{1,0:T(8,128)S(1)}, u32[]{:S(2)}, u32[]{:S(2)}) %collective-permute-start.5) | collective-permute-done | bytes 12320 | tf_op jit(solution)/shard_map/ppermute | solution.py:288
  40.7 0.1 join_y.1
  41.0 7.2 %collective-permute-start.7 = (f32[32,128]{1,0:T(8,128)S(1)}, f32[32,128]{1,0:T(8,128)S(1)}, u32[]{:S(2)}, u32[]{:S(2)}) collective-permute-start(f32[32,128]{1,0:T(8,128)S(1)} %get-tuple-element.70), channel_id=1, source_target_pairs={{16,32},{48,64},{80,96},{112,128},{144,160},{176,192},{208,224},{3... | collective-permute-start | bytes 49160 | tf_op jit(solution)/shard_map/ppermute | solution.py:288
  48.2 2.0 %collective-permute-done.7.rb = f32[32,128]{1,0:T(8,128)S(1)} collective-permute-done((f32[32,128]{1,0:T(8,128)S(1)}, f32[32,128]{1,0:T(8,128)S(1)}, u32[]{:S(2)}, u32[]{:S(2)}) %collective-permute-start.7) | collective-permute-done | bytes 16416 | tf_op jit(solution)/shard_map/ppermute | solution.py:288
  50.2 0.8 %finish.1 = f32[256,128]{1,0:T(8,128)} custom-call(f32[256,128]{1,0:T(8,128)S(1)} %get-tuple-element.68.core, f32[32,128]{1,0:T(8,128)S(1)} %collective-permute-done.6.ra, f32[32,128]{1,0:T(8,128)S(1)} %collective-permute-done.7.rb, f32[256,128]{1,0:T(8,128)S(1)} %bitcast.7, s32[32,128]{1,0:T(8,128)S(1)} %copy-done.5), custom_call_target="tpu_custom_call" | custom-call | flops 1000000 | bytes 1000000 | tf_op jit(solution)/shard_map/finish/pallas_call | solution.py:348
  (22 shorter events, 0.3 us)
Async XLA Ops:
  0.0 0.9 %copy-start.1 = (f32[8,32,128]{2,1,0:T(8,128)S(1)}, f32[8,32,128]{2,1,0:T(8,128)}, u32[]{:S(2)}) copy-start(f32[8,32,128]{2,1,0:T(8,128)} %param.9) | copy-start | bytes 393220
  0.9 0.7 %copy-start.3 = (s32[32,128]{1,0:T(8,128)S(1)}, s32[32,128]{1,0:T(8,128)}, u32[]{:S(2)}) copy-start(s32[32,128]{1,0:T(8,128)} %ac.5) | copy-start | bytes 49156
  1.6 0.8 %copy-start.6 = (bf16[8,32,128]{2,1,0:T(8,128)(2,1)S(1)}, bf16[8,32,128]{2,1,0:T(8,128)(2,1)}, u32[]{:S(2)}) copy-start(bf16[8,32,128]{2,1,0:T(8,128)(2,1)} %param.10) | copy-start | bytes 196612
  2.5 47.7 %copy-start.2 = (f32[8,32,128]{2,1,0:T(8,128)S(1)}, f32[8,32,128]{2,1,0:T(8,128)}, u32[]{:S(2)}) copy-start(f32[8,32,128]{2,1,0:T(8,128)} %param.9) | copy-start | bytes 393220
  2.5 47.7 %copy-start.5 = (s32[32,128]{1,0:T(8,128)S(1)}, s32[32,128]{1,0:T(8,128)}, u32[]{:S(2)}) copy-start(s32[32,128]{1,0:T(8,128)} %ac.5) | copy-start | bytes 49156
  2.6 9.5 %collective-permute-start = (f32[104,128]{1,0:T(8,128)S(1)}, f32[104,128]{1,0:T(8,128)S(1)}, u32[]{:S(2)}, u32[]{:S(2)}) collective-permute-start(f32[104,128]{1,0:T(8,128)S(1)} %get-tuple-element.40), channel_id=1, source_target_pairs={{0,16},{32,48},{64,80},{96,112},{128,144},{160,176},{192,208},{224... | collective-permute-start | bytes 159752 | tf_op jit(solution)/shard_map/ppermute | solution.py:288
  4.6 9.6 %collective-permute-start.1 = (f32[104,128]{1,0:T(8,128)S(1)}, f32[104,128]{1,0:T(8,128)S(1)}, u32[]{:S(2)}, u32[]{:S(2)}) collective-permute-start(f32[104,128]{1,0:T(8,128)S(1)} %get-tuple-element.41), channel_id=1, source_target_pairs={{16,32},{48,64},{80,96},{112,128},{144,160},{176,192},{208,224},{3... | collective-permute-start | bytes 159752 | tf_op jit(solution)/shard_map/ppermute | solution.py:288
  14.3 0.7 %copy-start.4 = (s32[32,128]{1,0:T(8,128)S(1)}, s32[32,128]{1,0:T(8,128)}, u32[]{:S(2)}) copy-start(s32[32,128]{1,0:T(8,128)} %ac.5) | copy-start | bytes 49156
  15.2 10.1 %collective-permute-start.2 = (f32[16,384]{1,0:T(8,128)S(1)}, f32[16,384]{1,0:T(8,128)S(1)}, u32[]{:S(2)}, u32[]{:S(2)}) collective-permute-start(f32[16,384]{1,0:T(8,128)S(1)} %get-tuple-element.44), channel_id=1, source_target_pairs={{0,1},{2,3},{4,5},{6,7},{8,9},{10,11},{12,13},{14,15},{1,0},{3,2},... | collective-permute-start | bytes 73736 | tf_op jit(solution)/shard_map/ppermute | solution.py:288
  15.3 10.1 %collective-permute-start.3 = (f32[16,384]{1,0:T(8,128)S(1)}, f32[16,384]{1,0:T(8,128)S(1)}, u32[]{:S(2)}, u32[]{:S(2)}) collective-permute-start(f32[16,384]{1,0:T(8,128)S(1)} %get-tuple-element.45), channel_id=1, source_target_pairs={{1,2},{3,4},{5,6},{7,8},{9,10},{11,12},{13,14},{2,1},{4,3},{6,5},{... | collective-permute-start | bytes 73736 | tf_op jit(solution)/shard_map/ppermute | solution.py:288
  20.2 0.7 %copy-start.7 = (f32[3,16,16]{2,1,0:T(8,128)S(1)}, f32[3,16,16]{2,1,0:T(8,128)}, u32[]{:S(2)}) copy-start(f32[3,16,16]{2,1,0:T(8,128)} %basis.1) | copy-start | bytes 9220
  21.0 0.7 %copy-start.8 = (s32[1,1,2]{2,1,0:T(1,128)S(1)}, s32[1,1,2]{2,1,0:T(1,128)}, u32[]{:S(2)}) copy-start(s32[1,1,2]{2,1,0:T(1,128)} %param.16) | copy-start | bytes 28
  21.6 0.7 %copy-start.9 = (f32[3,5]{1,0:T(4,128)S(1)}, f32[3,5]{1,0:T(4,128)}, u32[]{:S(2)}) copy-start(f32[3,5]{1,0:T(4,128)} %stiff.1) | copy-start | bytes 184
  22.3 0.7 %copy-start.10 = (f32[3,5]{1,0:T(4,128)S(1)}, f32[3,5]{1,0:T(4,128)}, u32[]{:S(2)}) copy-start(f32[3,5]{1,0:T(4,128)} %mass.1) | copy-start | bytes 184
  23.0 0.7 %copy-start.11 = (f32[3,16]{1,0:T(4,128)S(1)}, f32[3,16]{1,0:T(4,128)}, u32[]{:S(2)}) copy-start(f32[3,16]{1,0:T(4,128)} %values.1) | copy-start | bytes 580
  25.3 2.2 %copy-start = (bf16[1,1,2,16,256,256]{5,4,3,2,1,0:T(8,128)(2,1)S(1)}, bf16[1,1,2,16,256,256]{5,4,3,2,1,0:T(8,128)(2,1)}, u32[]{:S(2)}) copy-start(bf16[1,1,2,16,256,256]{5,4,3,2,1,0:T(8,128)(2,1)} %param.17) | copy-start | bytes 12582916
  33.5 2.9 %collective-permute-start.4 = (f32[8,384]{1,0:T(8,128)S(1)}, f32[8,384]{1,0:T(8,128)S(1)}, u32[]{:S(2)}, u32[]{:S(2)}) collective-permute-start(f32[8,384]{1,0:T(8,128)S(1)} %get-tuple-element.66), channel_id=1, source_target_pairs={{0,1},{2,3},{4,5},{6,7},{8,9},{10,11},{12,13},{14,15},{1,0},{3,2},... | collective-permute-start | bytes 36872 | tf_op jit(solution)/shard_map/ppermute | solution.py:288
  33.6 7.1 %collective-permute-start.5 = (f32[8,384]{1,0:T(8,128)S(1)}, f32[8,384]{1,0:T(8,128)S(1)}, u32[]{:S(2)}, u32[]{:S(2)}) collective-permute-start(f32[8,384]{1,0:T(8,128)S(1)} %get-tuple-element.67), channel_id=1, source_target_pairs={{1,2},{3,4},{5,6},{7,8},{9,10},{11,12},{13,14},{2,1},{4,3},{6,5},{... | collective-permute-start | bytes 36872 | tf_op jit(solution)/shard_map/ppermute | solution.py:288
  40.9 7.3 %collective-permute-start.6 = (f32[32,128]{1,0:T(8,128)S(1)}, f32[32,128]{1,0:T(8,128)S(1)}, u32[]{:S(2)}, u32[]{:S(2)}) collective-permute-start(f32[32,128]{1,0:T(8,128)S(1)} %get-tuple-element.69), channel_id=1, source_target_pairs={{0,16},{32,48},{64,80},{96,112},{128,144},{160,176},{192,208},{224... | collective-permute-start | bytes 49160 | tf_op jit(solution)/shard_map/ppermute | solution.py:288
  41.0 9.2 %collective-permute-start.7 = (f32[32,128]{1,0:T(8,128)S(1)}, f32[32,128]{1,0:T(8,128)S(1)}, u32[]{:S(2)}, u32[]{:S(2)}) collective-permute-start(f32[32,128]{1,0:T(8,128)S(1)} %get-tuple-element.70), channel_id=1, source_target_pairs={{16,32},{48,64},{80,96},{112,128},{144,160},{176,192},{208,224},{3... | collective-permute-start | bytes 49160 | tf_op jit(solution)/shard_map/ppermute | solution.py:288

commit v2 on v1

v2 whole, which is shorter than its diff:
```python
import functools

import jax
import jax.numpy as jnp
from jax import lax
from jax.experimental import pallas as pl
from jax.experimental.pallas import tpu as pltpu
from jax.sharding import PartitionSpec as P

BAND = 4
PATCH = 16
damping = 0.5
FAR = 100000

f32 = jnp.float32
bf16 = jnp.bfloat16
VMEM = pl.BlockSpec(memory_space=pltpu.VMEM)
ANY = pl.BlockSpec(memory_space=pl.ANY)


def split(x):
    hi = x.astype(bf16)
    return hi, (x - hi.astype(f32)).astype(bf16)


def split3(x):
    hi, rest = x.astype(bf16), x
    rest = rest - hi.astype(f32)
    mid = rest.astype(bf16)
    return hi, mid, (rest - mid.astype(f32)).astype(bf16)


def dot(a, b):
    return lax.dot_general(a, b, (((1,), (0,)), ((), ())), preferred_element_type=f32)


def dot_t(a, b):
    return lax.dot_general(a, b, (((1,), (1,)), ((), ())), preferred_element_type=f32)


def dot3(ah, al, bh, bl):
    return dot(ah, bh) + (dot(ah, bl) + dot(al, bh))


def pick(x, onehot):
    h, m, l = split3(x)
    return dot(h, onehot) + dot(m, onehot) + dot(l, onehot)


def place(onehot, x):
    h, m, l = split3(x)
    return dot(onehot, h) + dot(onehot, m) + dot(onehot, l)


def iota(shape, dim):
    return lax.broadcasted_iota(jnp.int32, shape, dim)


def parity(axis):
    return lax.rem(lax.axis_index(axis), 2)


def y_coord(lane, par):
    far = lane * 64 + FAR
    above, below = lane, lane - 136
    first = jnp.where(par == 0, above, below)
    second = jnp.where(par == 0, below - 8, above - 8)
    return jnp.where(
        lane < 128, lane, jnp.where(lane < 136, first, jnp.where(lane < 144, second, far))
    )


def toeplitz(dist, coeffs):
    out = jnp.zeros(dist.shape, f32)
    for k in range(BAND + 1):
        out = jnp.where(dist == k, coeffs[k], out)
    return out


def fetch(pairs, sem):
    copies = [pltpu.make_async_copy(a, b, sem.at[n]) for n, (a, b) in enumerate(pairs)]
    for copy in copies:
        copy.start()
    for copy in copies:
        copy.wait()


def either(flag, a, b):
    return jnp.where(flag == 0, a, b)


def pack_y_kernel(
    st_hbm, ld_hbm, ac_hbm, s_out, l_out, a_out, send_a, send_b, st, ld, ac, wide, sem
):
    fetch([(st_hbm, st), (ld_hbm, ld), (ac_hbm, ac)], sem)
    py = parity("gy")
    wide[...] = ld[...].astype(f32)
    for x in range(32):
        s_out[8 * x : 8 * x + 8, :] = st[pl.ds(x, 8, stride=32), :]
        l_out[8 * x : 8 * x + 8, :] = wide[pl.ds(x, 8, stride=32), :]
    act = ac[...].astype(f32)
    a_out[...] = act
    turned = [s_out[...].T, l_out[...].T, jnp.concatenate([act, jnp.zeros((96, 128), f32)], axis=0).T]
    low = jnp.concatenate([t[0:8] for t in turned], axis=1)
    high = jnp.concatenate([t[120:128] for t in turned], axis=1)
    send_a[...] = either(py, high, low)
    send_b[...] = either(py, low, high)


def pack_x_kernel(after, s, l, ac, ra, rb, sw, lw, aw, send_a, send_b):
    del after
    px = parity("gx")

    def strips(lanes, width):
        both = [ra[:, lanes], rb[:, lanes], jnp.zeros((112, width), f32)]
        return jnp.concatenate(both, axis=0).T

    sw[:, 0:128] = s[...]
    sw[:, 128:256] = strips(slice(0, 256), 256)
    lw[:, 0:128] = l[...]
    lw[:, 128:256] = strips(slice(256, 512), 256)
    aw[:, 0:128] = ac[...]
    aw[:, 128:256] = strips(slice(512, 640), 128)[0:32]

    def edge(srow, lrow, arow):
        rows = [sw[srow : srow + 64, :], lw[lrow : lrow + 32, :], aw[arow : arow + 8, :]]
        rows = jnp.concatenate(rows, axis=0)
        corner = jnp.concatenate([rows[:, 128:256], jnp.zeros((24, 128), f32)], axis=0).T
        return jnp.concatenate([rows[:, 0:128], corner[0:16]], axis=0)

    low, high = edge(0, 0, 0), edge(192, 224, 24)
    send_a[...] = either(px, high, low)
    send_b[...] = either(px, low, high)


def stencil(left_h, left_l, syh, syl, live, load):
    bh = jnp.concatenate([syh[:, 0:256], syh[:, 256:512]], axis=0)
    bl = jnp.concatenate([syl[:, 0:256], syl[:, 256:512]], axis=0)
    return split(live * (load - dot3(left_h, left_l, bh, bl)))


def solve_row(a, khl, kth, ktl, dinv, cols, ryh, ryl):
    modes = dot(khl, jnp.concatenate([ryh, ryh], axis=0)) + dot(khl[:, 0:128], ryl)
    lane_b = iota((1, 256), 1) >> 4
    keep = jnp.ones((1, 256), f32)
    for m in range(2):
        keep = jnp.where(lane_b + 16 * a == cols[m], 0.0, keep)
    mh, ml = split(modes * dinv * keep)
    return dot3(kth, ktl, mh, ml)


def inner_kernel(
    cols_hbm, sw, lw, aw, yh, yl, lh, ll, ayh, ayl, khl, kth, ktl, dinv, inverse,
    syh, syl, rh, rl, ryh, ryl, tin, inv, cols, sem,
):
    listed = pltpu.make_async_copy(cols_hbm, cols, sem.at[2])
    listed.start()
    copies = [pltpu.make_async_copy(inverse.at[m], inv.at[m], sem.at[m]) for m in range(2)]
    for copy in copies:
        copy.start()
    sh, sl = split(sw[...])
    syh[...], syl[...] = split(dot3(sh, sl, yh[...], yl[...]))
    spread = jnp.where((iota((192, 32), 0) >> 3) + 4 == iota((192, 32), 1), 1.0, 0.0)
    live = dot(spread.astype(bf16), aw[...].astype(bf16))
    for o in range(3):
        rows, mine = slice(64 * o, 64 * o + 128), slice(64 * o, 64 * o + 64)
        load = lw[64 * o + 32 : 64 * o + 96, :]
        rh[mine, :], rl[mine, :] = stencil(
            lh[...], ll[...], syh[rows, :], syl[rows, :], live[mine], load
        )
    ryh[...], ryl[...] = split(dot3(rh[...], rl[...], ayh[...], ayl[...]))
    listed.wait()
    rest = (khl[...], kth[...], ktl[...], dinv[...], cols)
    one = solve_row(1, *rest, ryh[0:128, :], ryl[0:128, :])
    two = solve_row(2, *rest, ryh[64:192, :], ryl[64:192, :])
    tin[0:64, :] = one[0:64]
    tin[64:128, :] = one[64:128] + two[0:64]
    tin[128:192, :] = two[64:128]
    for copy in copies:
        copy.wait()


def edge_kernel(
    cols_hbm, lw, aw, ra, rb, syh, syl, rh_in, rl_in, ryh, ryl, inv,
    yh, yl, lh, ll, ayh, ayl, ath, atl, khl, kth, ktl, dinv, sel, sel_t, lzh, lzl, lzth, lztl,
    first, last, cut, send_a, send_b, rh, rl, cols, sem,
):
    listed = pltpu.make_async_copy(cols_hbm, cols, sem)
    listed.start()
    px = parity("gx")
    low, high = either(px, rb[...], ra[...]), either(px, ra[...], rb[...])

    def halo(block):
        corner = jnp.concatenate([block[104:120], jnp.zeros((112, 128), f32)], axis=0).T
        return jnp.concatenate([block[0:104], corner[0:104]], axis=1)

    low, high = halo(low), halo(high)
    sh, sl = split(jnp.concatenate([low[0:64], high[0:64]], axis=0))
    ehh, ehl = split(dot3(sh, sl, yh[...], yl[...]))
    spread = jnp.where((iota((64, 16), 0) >> 3) + 4 == iota((64, 16), 1), 1.0, 0.0).astype(bf16)
    rh[64:256, :], rl[64:256, :] = rh_in[...], rl_in[...]
    live = dot(spread, jnp.concatenate([low[96:104], aw[0:8, :]], axis=0).astype(bf16))
    rh[0:64, :], rl[0:64, :] = stencil(
        lh[...],
        ll[...],
        jnp.concatenate([ehh[0:64], syh[0:64, :]], axis=0),
        jnp.concatenate([ehl[0:64], syl[0:64, :]], axis=0),
        live,
        jnp.concatenate([low[64:96], lw[0:32, :]], axis=0),
    )
    live = dot(spread, jnp.concatenate([aw[24:32, :], high[96:104]], axis=0).astype(bf16))
    rh[256:320, :], rl[256:320, :] = stencil(
        lh[...],
        ll[...],
        jnp.concatenate([syh[192:256, :], ehh[64:128]], axis=0),
        jnp.concatenate([syl[192:256, :], ehl[64:128]], axis=0),
        live,
        jnp.concatenate([lw[224:256, :], high[64:96]], axis=0),
    )
    same = (iota((128, 256), 0) >> 3) == (iota((128, 256), 1) >> 4)
    row_k = iota((16, 256), 0)
    listed.wait()
    cut[...] = jnp.zeros((320, 256), f32)
    for m in range(2):
        at = pl.multiple_of(64 * (jnp.maximum(cols[m], 0) >> 4), 64)
        rows = pl.ds(at, 128)
        cells = dot(rh[rows, :], sel[m]) + dot(rl[rows, :], sel[m])
        ch, cl = split(jnp.where(same, cells, 0.0))
        zmodes = dot3(lzh[...], lzl[...], ch, cl)
        dense = jnp.zeros((16, 256), f32)
        for k in range(16):
            single = jnp.where(row_k == k, zmodes, 0.0).astype(bf16)
            dense = dense + dot_t(single, inv[m, k])
        dh, dl = split(dense)
        back = dot3(lzth[...], lztl[...], dh, dl)
        gh, gl = split(jnp.where(same, back, 0.0))
        cut[rows, :] += dot(gh, sel_t[m]) + dot(gl, sel_t[m])
    edges_h = jnp.concatenate([rh[0:64, :], rh[256:320, :]], axis=0)
    edges_l = jnp.concatenate([rl[0:64, :], rl[256:320, :]], axis=0)
    eyh, eyl = split(dot3(edges_h, edges_l, ayh[...], ayl[...]))
    rest = (khl[...], kth[...], ktl[...], dinv[...], cols)
    t0 = solve_row(
        0,
        *rest,
        jnp.concatenate([eyh[0:64], ryh[0:64, :]], axis=0),
        jnp.concatenate([eyl[0:64], ryl[0:64, :]], axis=0),
    )
    t3 = solve_row(
        3,
        *rest,
        jnp.concatenate([ryh[128:192, :], eyh[64:128]], axis=0),
        jnp.concatenate([ryl[128:192, :], eyl[64:128]], axis=0),
    )
    first[...], last[...] = t0[32:128], t3[0:96]
    th, tl = split(jnp.concatenate([t0[0:32], t3[96:128]], axis=0))
    out = dot3(th, tl, ath[...], atl[...])
    out_low, out_high = out[0:32] + cut[0:32, :], out[32:64] + cut[288:320, :]
    pad = jnp.zeros((96, 128), f32)
    corner_low = jnp.concatenate([pad, out_low[:, 128:256]], axis=0).T
    corner_high = jnp.concatenate([out_high[:, 128:256], pad], axis=0).T
    out_low = jnp.concatenate([out_low[:, 0:128], corner_low[0:16]], axis=0)
    out_high = jnp.concatenate([out_high[:, 0:128], corner_high[0:16]], axis=0)
    send_a[...] = either(px, out_high, out_low)
    send_b[...] = either(px, out_low, out_high)


def spread_kernel(first, last, tin, cut, ath, atl, core, side):
    total = jnp.concatenate(
        [
            first[0:32, :],
            first[32:96, :] + tin[0:64, :],
            tin[64:128, :],
            tin[128:192, :] + last[0:64, :],
            last[64:96, :],
        ],
        axis=0,
    )
    th, tl = split(total)
    total = dot3(th, tl, ath[...], atl[...]) + cut[32:288, :]
    core[...] = total[:, 0:128]
    side[...] = total[:, 128:256].T[0:16]


def join_x_kernel(side, ra, rb, send_a, send_b):
    px = parity("gx")
    low, high = either(px, rb[32:48, :], ra[32:48, :]), either(px, ra[32:48, :], rb[32:48, :])
    full = side[...] + jnp.concatenate([low, high], axis=1)
    send_a[...] = full[0:8]
    send_b[...] = full[8:16]


def finish_kernel(core, xa, xb, ya, yb, s, ac, out):
    px, py = parity("gx"), parity("gy")
    low, high = either(px, xb[0:32, :], xa[0:32, :]), either(px, xa[0:32, :], xb[0:32, :])
    left, right = either(py, yb[...], ya[...]), either(py, ya[...], yb[...])
    edge = jnp.concatenate([left, jnp.zeros((112, 256), f32), right], axis=0).T
    total = core[...] + edge
    for x in range(32):
        term = total[8 * x : 8 * x + 8]
        if x < 4:
            term = term + low[8 * x : 8 * x + 8]
        if x >= 28:
            term = term + high[8 * (x - 28) : 8 * (x - 28) + 8]
        row = damping * ac[pl.ds(x, 1), :]
        out[pl.ds(x, 8, stride=32), :] = s[8 * x : 8 * x + 8, :] + row * term


def build_kernel(
    after, stiff_hbm, mass_hbm, basis_hbm, values_hbm, cols_hbm,
    yh, yl, lh, ll, ayh, ayl, ath, atl, khl, kth, ktl, dinv, sel, sel_t, lzh, lzl, lzth, lztl,
    stiff, mass, basis, values, cols, sem,
):
    del after
    fetch(
        [
            (stiff_hbm, stiff),
            (mass_hbm, mass),
            (basis_hbm, basis),
            (values_hbm, values),
            (cols_hbm, cols),
        ],
        sem,
    )
    py = parity("gy")
    kz, kx, ky = ([stiff[d, k] for k in range(BAND + 1)] for d in range(3))
    mz, mx, my = ([mass[d, k] for k in range(BAND + 1)] for d in range(3))
    dist = jnp.abs(y_coord(iota((256, 256), 0), py) - y_coord(iota((256, 256), 1), py))
    yh[:, 0:256], yl[:, 0:256] = split(toeplitz(dist, my))
    yh[:, 256:512], yl[:, 256:512] = split(toeplitz(dist, ky))
    row, col = iota((64, 128), 0), iota((64, 128), 1)
    dx = jnp.abs((row >> 3) + 4 - (col >> 3))
    dz = jnp.abs((row & 7) - (col & 7))
    tmz, tmx = toeplitz(dz, mz), toeplitz(dx, mx)
    first = tmz * toeplitz(dx, kx) + toeplitz(dz, kz) * tmx
    lh[:, 0:128], ll[:, 0:128] = split(first)
    lh[:, 128:256], ll[:, 128:256] = split(tmz * tmx)
    one = lambda cond: jnp.where(cond, 1.0, 0.0).astype(bf16)
    tile_j = one(iota((16, 256), 0) == (iota((16, 256), 1) & 15))
    vy = pick(basis[2], tile_j)
    c = y_coord(iota((256, 256), 0), py)
    b = iota((256, 256), 1) >> 4
    t = c + 4 - 8 * b
    lower = jnp.concatenate([vy[4:8], vy[0:4]], axis=0)
    upper = jnp.concatenate([vy[12:16], vy[8:12]], axis=0)
    lower = jnp.concatenate([lower] * 32, axis=0)
    upper = jnp.concatenate([upper] * 32, axis=0)
    ay = jnp.where((t >= 0) & (t < 8), lower, jnp.where((t >= 8) & (t < 16), upper, 0.0))
    ayh[...], ayl[...] = split(ay)
    ath[...], atl[...] = split(ay.T)
    to_i = one((iota((256, 16), 0) >> 4) == iota((256, 16), 1))
    to_k = one((iota((256, 16), 0) & 15) == iota((256, 16), 1))
    to_xx = one((iota((16, 128), 1) >> 3) == iota((16, 128), 0))
    to_z = one((iota((16, 128), 1) & 7) + 4 == iota((16, 128), 0))
    vz_rows = pick(basis[0].T, to_z)
    vx_rows = pick(basis[1].T, to_xx)
    kron = place(to_i, vx_rows) * place(to_k, vz_rows)
    khl[:, 0:128], khl[:, 128:256] = split(kron)
    kth[...], ktl[...] = split(kron.T)
    lzh[...], lzl[...] = split(vz_rows)
    lzth[...], lztl[...] = split(vz_rows.T)
    lam = values[...]
    lanes = pick(jnp.concatenate([lam, jnp.zeros((5, 16), f32)], axis=0), tile_j)[2:3]
    lam_t = jnp.concatenate([lam, jnp.zeros((5, 16), f32)], axis=0).T
    lam_i, lam_k = place(to_i, lam_t)[:, 1:2], place(to_k, lam_t)[:, 0:1]
    dinv[...] = 1.0 / (lam_k + lam_i + lanes)
    yy = iota((256, 256), 1) & 15
    cy = y_coord(iota((256, 256), 0), py)
    yy_t = iota((256, 256), 0) & 15
    cy_t = y_coord(iota((256, 256), 1), py)
    for m in range(2):
        entry = cols[m]
        at = jnp.where(entry >= 0, 8 * (jnp.maximum(entry, 0) & 15) - 4, -4 * FAR)
        sel[m] = one(cy == yy + at)
        sel_t[m] = one(cy_t == yy_t + at)


def call(kernel, outs, ins, scratch=(), name=None, flops=10**6, limit=8 * 2**20):
    return pl.pallas_call(
        kernel,
        out_shape=[jax.ShapeDtypeStruct(s, t) for s, t in outs],
        in_specs=ins,
        out_specs=[VMEM] * len(outs),
        scratch_shapes=scratch,
        name=name,
        compiler_params=pltpu.CompilerParams(vmem_limit_bytes=limit),
        cost_estimate=pl.CostEstimate(flops=flops, bytes_accessed=10**6, transcendentals=0),
    )


def swaps(axis, first):
    size = lax.axis_size(axis)
    lows = range(first, size - 1, 2)
    return [(i, i + 1) for i in lows] + [(i + 1, i) for i in lows]


def exchange(a, b, axis):
    return lax.ppermute(a, axis, swaps(axis, 0)), lax.ppermute(b, axis, swaps(axis, 1))


def on_device(
    state, load_vector, active, stiff_band, mass_band, eig_basis, eig_values, cut_cols, cut_inverse
):
    st, ld, active, stiff, mass, basis, values, cols_in, inverse = (
        pltpu.with_memory_space_constraint(x, pltpu.HBM)
        for x in (
            state.reshape(256, 128),
            load_vector.reshape(256, 128),
            active,
            stiff_band,
            mass_band,
            eig_basis,
            eig_values,
            cut_cols.reshape(2),
            cut_inverse.reshape(2, PATCH, 256, 256),
        )
    )
    dma = pltpu.SemaphoreType.DMA
    s, l, ac, ya, yb = call(
        pack_y_kernel,
        [((256, 128), f32), ((256, 128), f32), ((32, 128), f32), ((8, 640), f32), ((8, 640), f32)],
        [ANY] * 3,
        [
            pltpu.VMEM((256, 128), f32),
            pltpu.VMEM((256, 128), bf16),
            pltpu.VMEM((32, 128), jnp.int32),
            pltpu.VMEM((256, 128), f32),
            dma((3,)),
        ],
        name="pack_y",
        limit=8 * 2**20,
    )(st, ld, active)
    ya, yb = exchange(ya, yb, "gy")
    sq = ((256, 256), bf16)
    yh, yl, lh, ll, ayh, ayl, ath, atl, khl, kth, ktl, dinv, *cutters = call(
        build_kernel,
        [
            ((256, 512), bf16), ((256, 512), bf16), ((64, 256), bf16), ((64, 256), bf16),
            sq, sq, sq, sq,
            sq, ((128, 256), bf16), ((128, 256), bf16),
            ((256, 256), f32), ((2, 256, 256), bf16), ((2, 256, 256), bf16),
            ((16, 128), bf16), ((16, 128), bf16), ((128, 16), bf16), ((128, 16), bf16),
        ],
        [VMEM] + [ANY] * 5,
        [
            pltpu.SMEM((3, 5), f32),
            pltpu.SMEM((3, 5), f32),
            pltpu.VMEM((3, 16, 16), f32),
            pltpu.VMEM((3, 16), f32),
            pltpu.SMEM((2,), jnp.int32),
            dma((5,)),
        ],
        name="build",
        limit=8 * 2**20,
    )(ac, stiff, mass, basis, values, cols_in)
    sw, lw, aw, xa, xb = call(
        pack_x_kernel,
        [((256, 256), f32), ((256, 256), f32), ((32, 256), f32), ((120, 128), f32), ((120, 128), f32)],
        [VMEM] * 6,
        name="pack_x",
    )(lh, s, l, ac, ya, yb)
    xa, xb = exchange(xa, xb, "gx")
    syh, syl, rh, rl, ryh, ryl, tin, inv = call(
        inner_kernel,
        [
            ((256, 512), bf16), ((256, 512), bf16),
            ((192, 256), bf16), ((192, 256), bf16), ((192, 256), bf16), ((192, 256), bf16),
            ((192, 256), f32), ((2, PATCH, 256, 256), bf16),
        ],
        [ANY] + [VMEM] * 13 + [ANY],
        [pltpu.SMEM((2,), jnp.int32), dma((3,))],
        name="inner",
        limit=12 * 2**20,
    )(cols_in, sw, lw, aw, yh, yl, lh, ll, ayh, ayl, khl, kth, ktl, dinv, inverse)
    first, last, cut, xa, xb = call(
        edge_kernel,
        [
            ((96, 256), f32), ((96, 256), f32), ((320, 256), f32),
            ((48, 128), f32), ((48, 128), f32),
        ],
        [ANY] + [VMEM] * 29,
        [
            pltpu.VMEM((320, 256), bf16),
            pltpu.VMEM((320, 256), bf16),
            pltpu.SMEM((2,), jnp.int32),
            dma,
        ],
        name="edge",
    )(
        cols_in, lw, aw, xa, xb, syh, syl, rh, rl, ryh, ryl, inv,
        yh, yl, lh, ll, ayh, ayl, ath, atl, khl, kth, ktl, dinv, *cutters,
    )
    xa, xb = exchange(xa, xb, "gx")
    core, side = call(
        spread_kernel, [((256, 128), f32), ((16, 256), f32)], [VMEM] * 6, name="spread"
    )(first, last, tin, cut, ath, atl)
    ya, yb = call(
        join_x_kernel, [((8, 256), f32), ((8, 256), f32)], [VMEM] * 3, name="join_x"
    )(side, xa, xb)
    ya, yb = exchange(ya, yb, "gy")
    (out,) = call(finish_kernel, [((256, 128), f32)], [VMEM] * 7, name="finish")(
        core, xa, xb, ya, yb, s, ac
    )
    return out.reshape(8, 32, 128)


def solution(mesh):
    placed = (
        P(None, "gx", "gy"),
        P(None, "gx", "gy"),
        P("gx", "gy"),
        P(),
        P(),
        P(),
        P(),
        P("gx", "gy", None),
        P("gx", "gy", None, None, None, None),
    )
    return jax.shard_map(
        on_device, mesh=mesh, in_specs=placed, out_specs=P(None, "gx", "gy"), check_vma=False
    )
```

time: 51.6 us -> 44.2 us (0.86)
  local copies, waits for them, and re-layouts: 8.8 us -> 0 us
  Pallas kernels: 8.91 us -> 12.8 us
  starting transfers between devices: 24.8 us -> 23.7 us
  waiting for transfers between devices: 8.39 us -> 7.34 us
    unnamed x24 -> x0, local copies, waits for them, and re-layouts: 8.8 us -> none
    pallas_call x5 -> x7, Pallas kernels: 7.27 us -> 10.9 us  [the longest x1 5.44 us: on_device(): call(edge_kernel, [((96, 256), f32), ((96, 256), f32), ((320, 256), f32),...]
    ppermute x4, waiting for transfers between devices: 8.38 us -> 7.33 us  [exchange(): lax.ppermute(b, axis, swaps(axis, 1))]
    ppermute x4, starting transfers between devices: 22.5 us -> 21.5 us  [exchange(): lax.ppermute(b, axis, swaps(axis, 1))]
  transfers between devices with their start and end apart: 8 -> 8, of which waited for: 3 -> 3; matrix products, arithmetic and copies ran while one was open for 0% -> 0% of each run, Pallas kernels for 3% -> 12%
where the time goes in v2:
time: 44.2 us; the launch traced here: 44 us
  starting transfers between devices  23.7 us (54%)
  Pallas kernels  12.8 us (29%)
  waiting for transfers between devices  7.34 us (17%)
    ppermute x4, starting transfers between devices, exchange(): lax.ppermute(b, axis, swaps(axis, 1))  21.5 us
    ppermute x4, waiting for transfers between devices, exchange(): lax.ppermute(b, axis, swaps(axis, 1))  7.33 us
    pallas_call x1, Pallas kernels, on_device(): call(edge_kernel, [((96, 256), f32), ((96, 256), f32), ((320, 256), f32),...  5.44 us
    pallas_call x1, Pallas kernels, on_device(): call(inner_kernel, [((256, 512), bf16), ((256, 512), bf16), ((192, 256),...  2.93 us
    ppermute x4, starting transfers between devices, exchange(): lax.ppermute(a, axis, swaps(axis, 0))  2.16 us
    pallas_call x1, Pallas kernels, on_device(): call(build_kernel, [((256, 512), bf16), ((256, 512), bf16), ((64, 256), b...  1.94 us
    pallas_call x1, Pallas kernels, on_device(): call(pack_y_kernel, [((256, 128), f32), ((256, 128), f32), ((32, 128), f3...  1.2 us
  transfers between devices with their start and end apart: 8, of which 3 were waited for; matrix products, arithmetic and copies ran while one was open for 0% of the time, Pallas kernels for 12%

profile of v2, /device:TPU:24, one launch (start us, length us, event | category | flops | bytes accessed | tf_op | source)
XLA Modules:
  0.0 44.0 jit_solution(18178183305814462364)
XLA Ops:
  0.0 1.2 %pack_y.1 = (f32[256,128]{1,0:T(8,128)S(1)}, f32[256,128]{1,0:T(8,128)S(1)}, f32[32,128]{1,0:T(8,128)S(1)}, f32[8,640]{1,0:T(8,128)S(1)}, f32[8,640]{1,0:T(8,128)S(1)}) custom-call(f32[256,128]{1,0:T(8,128)} %bitcast.6, bf16[256,128]{1,0:T(8,128)(2,1)} %bitcast.7, s32[32,128]{1,0:T(8,128)} %ac_hbm.1), custom_call_target="tpu_custom_call" | custom-call | flops 1000000 | bytes 1000000 | tf_op jit(solution)/shard_map/pack_y/pallas_call | solution.py:418
  1.2 0.1 collective-permute-start
  1.3 4.9 %collective-permute-start.1 = (f32[8,640]{1,0:T(8,128)S(1)}, f32[8,640]{1,0:T(8,128)S(1)}, u32[]{:S(2)}, u32[]{:S(2)}) collective-permute-start(f32[8,640]{1,0:T(8,128)S(1)} %get-tuple-element.55), channel_id=1, source_target_pairs={{1,2},{3,4},{5,6},{7,8},{9,10},{11,12},{13,14},{2,1},{4,3},{6,5},{... | collective-permute-start | bytes 61448 | tf_op jit(solution)/shard_map/ppermute | solution.py:397
  6.2 1.9 %build.1 = (bf16[256,512]{1,0:T(8,128)(2,1)S(1)}, bf16[256,512]{1,0:T(8,128)(2,1)S(1)}, bf16[64,256]{1,0:T(8,128)(2,1)S(1)}, bf16[64,256]{1,0:T(8,128)(2,1)S(1)}...) custom-call(f32[32,128]{1,0:T(8,128)S(1)} %get-tuple-element.50.afte, ...), custom_call_target="tpu_custom_call" | custom-call | flops 1000000 | bytes 1000000 | tf_op jit(solution)/shard_map/build/pallas_call | solution.py:434
  8.2 0.0 collective-permute-done.ra
  8.2 0.3 collective-permute-done.1.rb
  8.5 0.2 pack_x.1
  8.7 2.0 %collective-permute-start.2 = (f32[120,128]{1,0:T(8,128)S(1)}, f32[120,128]{1,0:T(8,128)S(1)}, u32[]{:S(2)}, u32[]{:S(2)}) collective-permute-start(f32[120,128]{1,0:T(8,128)S(1)} %get-tuple-element.58), channel_id=1, source_target_pairs={{0,16},{32,48},{64,80},{96,112},{128,144},{160,176},{192,208},{224... | collective-permute-start | bytes 184328 | tf_op jit(solution)/shard_map/ppermute | solution.py:397
  10.7 7.5 %collective-permute-start.3 = (f32[120,128]{1,0:T(8,128)S(1)}, f32[120,128]{1,0:T(8,128)S(1)}, u32[]{:S(2)}, u32[]{:S(2)}) collective-permute-start(f32[120,128]{1,0:T(8,128)S(1)} %get-tuple-element.59), channel_id=1, source_target_pairs={{16,32},{48,64},{80,96},{112,128},{144,160},{176,192},{208,224},{3... | collective-permute-start | bytes 184328 | tf_op jit(solution)/shard_map/ppermute | solution.py:397
  18.2 2.9 %inner.1 = (bf16[256,512]{1,0:T(8,128)(2,1)S(1)}, bf16[256,512]{1,0:T(8,128)(2,1)S(1)}, bf16[192,256]{1,0:T(8,128)(2,1)S(1)}, bf16[192,256]{1,0:T(8,128)(2,1)S(1...) custom-call(s32[2]{0:T(128)} %bitcast.9, ...), custom_call_target="tpu_custom_call" | custom-call | flops 1000000 | bytes 1000000 | tf_op jit(solution)/shard_map/inner/pallas_call | solution.py:462
  21.1 0.0 collective-permute-done.2.ra
  21.1 0.0 collective-permute-done.3.rb
  21.2 5.4 %edge.1 = (f32[96,256]{1,0:T(8,128)S(1)}, f32[96,256]{1,0:T(8,128)S(1)}, f32[320,256]{1,0:T(8,128)S(1)}, f32[48,128]{1,0:T(8,128)S(1)}, f32[48,128]{1,0:T(8,128)S(1)}) custom-call(s32[2]{0:T(128)} %bitcast.10, f32[256,256]{1,0:T(8,128)S(1)} %get-tuple-element.56.lw, f32[32,256]{1,0:T(8,128)S(1)} %get-tuple-element.57.aw, ...), custom_call_target="tpu_custom_call" | custom-call | flops 1000000 | bytes 1000000 | tf_op jit(solution)/shard_map/edge/pallas_call | solution.py:474
  26.6 0.1 collective-permute-start.4
  26.7 6.7 %collective-permute-start.5 = (f32[48,128]{1,0:T(8,128)S(1)}, f32[48,128]{1,0:T(8,128)S(1)}, u32[]{:S(2)}, u32[]{:S(2)}) collective-permute-start(f32[48,128]{1,0:T(8,128)S(1)} %get-tuple-element.91), channel_id=1, source_target_pairs={{16,32},{48,64},{80,96},{112,128},{144,160},{176,192},{208,224},{3... | collective-permute-start | bytes 73736 | tf_op jit(solution)/shard_map/ppermute | solution.py:397
  33.4 0.3 spread.1
  33.8 0.0 collective-permute-done.4.ra.xa
  33.8 2.3 %collective-permute-done.5.rb.xb = f32[48,128]{1,0:T(8,128)S(1)} collective-permute-done((f32[48,128]{1,0:T(8,128)S(1)}, f32[48,128]{1,0:T(8,128)S(1)}, u32[]{:S(2)}, u32[]{:S(2)}) %collective-permute-start.5) | collective-permute-done | bytes 24608 | tf_op jit(solution)/shard_map/ppermute | solution.py:397
  36.0 0.0 collective-permute-start.6
  36.1 2.3 %collective-permute-start.7 = (f32[8,256]{1,0:T(8,128)S(1)}, f32[8,256]{1,0:T(8,128)S(1)}, u32[]{:S(2)}, u32[]{:S(2)}) collective-permute-start(f32[8,256]{1,0:T(8,128)S(1)} %get-tuple-element.94), channel_id=1, source_target_pairs={{1,2},{3,4},{5,6},{7,8},{9,10},{11,12},{13,14},{2,1},{4,3},{6,5},{... | collective-permute-start | bytes 24584 | tf_op jit(solution)/shard_map/ppermute | solution.py:397
  38.4 0.0 collective-permute-done.6.ya
  38.4 4.7 %collective-permute-done.7.yb = f32[8,256]{1,0:T(8,128)S(1)} collective-permute-done((f32[8,256]{1,0:T(8,128)S(1)}, f32[8,256]{1,0:T(8,128)S(1)}, u32[]{:S(2)}, u32[]{:S(2)}) %collective-permute-start.7) | collective-permute-done | bytes 8224 | tf_op jit(solution)/shard_map/ppermute | solution.py:397
  43.1 0.8 %finish.1 = f32[256,128]{1,0:T(8,128)} custom-call(f32[256,128]{1,0:T(8,128)S(1)} %get-tuple-element.89.core, f32[48,128]{1,0:T(8,128)S(1)} %collective-permute-done.4.ra.xa, f32[48,128]{1,0:T(8,128)S(1)} %collective-permute-done.5.rb.xb, f32[8,256]{1,0:T(8,128)S(1)} %collective-permute-done.6.ya, f32[8,256]{1,0:T(8,128)S(1)} %collective-permute-done.7.yb, ...), custom_call_target="tpu_custom_call" | custom-call | flops 1000000 | bytes 1000000 | tf_op jit(solution)/shard_map/finish/pallas_call | solution.py:500
  (1 shorter events, 0.0 us)
Async XLA Ops:
  1.2 7.0 %collective-permute-start = (f32[8,640]{1,0:T(8,128)S(1)}, f32[8,640]{1,0:T(8,128)S(1)}, u32[]{:S(2)}, u32[]{:S(2)}) collective-permute-start(f32[8,640]{1,0:T(8,128)S(1)} %get-tuple-element.54), channel_id=1, source_target_pairs={{0,1},{2,3},{4,5},{6,7},{8,9},{10,11},{12,13},{14,15},{1,0},{3,2},... | collective-permute-start | bytes 61448 | tf_op jit(solution)/shard_map/ppermute | solution.py:397
  1.3 7.2 %collective-permute-start.1 = (f32[8,640]{1,0:T(8,128)S(1)}, f32[8,640]{1,0:T(8,128)S(1)}, u32[]{:S(2)}, u32[]{:S(2)}) collective-permute-start(f32[8,640]{1,0:T(8,128)S(1)} %get-tuple-element.55), channel_id=1, source_target_pairs={{1,2},{3,4},{5,6},{7,8},{9,10},{11,12},{13,14},{2,1},{4,3},{6,5},{... | collective-permute-start | bytes 61448 | tf_op jit(solution)/shard_map/ppermute | solution.py:397
  8.7 12.4 %collective-permute-start.2 = (f32[120,128]{1,0:T(8,128)S(1)}, f32[120,128]{1,0:T(8,128)S(1)}, u32[]{:S(2)}, u32[]{:S(2)}) collective-permute-start(f32[120,128]{1,0:T(8,128)S(1)} %get-tuple-element.58), channel_id=1, source_target_pairs={{0,16},{32,48},{64,80},{96,112},{128,144},{160,176},{192,208},{224... | collective-permute-start | bytes 184328 | tf_op jit(solution)/shard_map/ppermute | solution.py:397
  10.7 10.5 %collective-permute-start.3 = (f32[120,128]{1,0:T(8,128)S(1)}, f32[120,128]{1,0:T(8,128)S(1)}, u32[]{:S(2)}, u32[]{:S(2)}) collective-permute-start(f32[120,128]{1,0:T(8,128)S(1)} %get-tuple-element.59), channel_id=1, source_target_pairs={{16,32},{48,64},{80,96},{112,128},{144,160},{176,192},{208,224},{3... | collective-permute-start | bytes 184328 | tf_op jit(solution)/shard_map/ppermute | solution.py:397
  26.6 7.2 %collective-permute-start.4 = (f32[48,128]{1,0:T(8,128)S(1)}, f32[48,128]{1,0:T(8,128)S(1)}, u32[]{:S(2)}, u32[]{:S(2)}) collective-permute-start(f32[48,128]{1,0:T(8,128)S(1)} %get-tuple-element.90), channel_id=1, source_target_pairs={{0,16},{32,48},{64,80},{96,112},{128,144},{160,176},{192,208},{224... | collective-permute-start | bytes 73736 | tf_op jit(solution)/shard_map/ppermute | solution.py:397
  26.7 9.3 %collective-permute-start.5 = (f32[48,128]{1,0:T(8,128)S(1)}, f32[48,128]{1,0:T(8,128)S(1)}, u32[]{:S(2)}, u32[]{:S(2)}) collective-permute-start(f32[48,128]{1,0:T(8,128)S(1)} %get-tuple-element.91), channel_id=1, source_target_pairs={{16,32},{48,64},{80,96},{112,128},{144,160},{176,192},{208,224},{3... | collective-permute-start | bytes 73736 | tf_op jit(solution)/shard_map/ppermute | solution.py:397
  36.0 2.3 %collective-permute-start.6 = (f32[8,256]{1,0:T(8,128)S(1)}, f32[8,256]{1,0:T(8,128)S(1)}, u32[]{:S(2)}, u32[]{:S(2)}) collective-permute-start(f32[8,256]{1,0:T(8,128)S(1)} %get-tuple-element.93), channel_id=1, source_target_pairs={{0,1},{2,3},{4,5},{6,7},{8,9},{10,11},{12,13},{14,15},{1,0},{3,2},... | collective-permute-start | bytes 24584 | tf_op jit(solution)/shard_map/ppermute | solution.py:397
  36.1 7.1 %collective-permute-start.7 = (f32[8,256]{1,0:T(8,128)S(1)}, f32[8,256]{1,0:T(8,128)S(1)}, u32[]{:S(2)}, u32[]{:S(2)}) collective-permute-start(f32[8,256]{1,0:T(8,128)S(1)} %get-tuple-element.94), channel_id=1, source_target_pairs={{1,2},{3,4},{5,6},{7,8},{9,10},{11,12},{13,14},{2,1},{4,3},{6,5},{... | collective-permute-start | bytes 24584 | tf_op jit(solution)/shard_map/ppermute | solution.py:397

commit v3 on v2

--- a/solution.py
+++ b/solution.py
@@ -139,54 +139,99 @@
     return split(live * (load - dot3(left_h, left_l, bh, bl)))
 
 
-def solve_row(a, khl, kth, ktl, dinv, cols, ryh, ryl):
+def solve_row(a, khl, kth, ktl, dinv, listed, ryh, ryl):
     modes = dot(khl, jnp.concatenate([ryh, ryh], axis=0)) + dot(khl[:, 0:128], ryl)
     lane_b = iota((1, 256), 1) >> 4
     keep = jnp.ones((1, 256), f32)
     for m in range(2):
-        keep = jnp.where(lane_b + 16 * a == cols[m], 0.0, keep)
+        entry = jnp.concatenate([listed[8 * m : 8 * m + 1]] * 2, axis=1)
+        keep = jnp.where(lane_b + 16 * a == entry, 0.0, keep)
     mh, ml = split(modes * dinv * keep)
     return dot3(kth, ktl, mh, ml)
 
 
-def inner_kernel(
-    cols_hbm, sw, lw, aw, yh, yl, lh, ll, ayh, ayl, khl, kth, ktl, dinv, inverse,
-    syh, syl, rh, rl, ryh, ryl, tin, inv, cols, sem,
+def column_cells(rows, rh, rl, sel, lzh, lzl, same):
+    cells = dot(rh[rows, :], sel) + dot(rl[rows, :], sel)
+    ch, cl = split(jnp.where(same, cells, 0.0))
+    return dot3(lzh, lzl, ch, cl)
+
+
+def cut_column(m, here, entry, rh, rl, sel, sel_t, lzh, lzl, lzth, lztl, inv, cut):
+    @pl.when((entry >= 0) & here)
+    def _():
+        same = (iota((128, 256), 0) >> 3) == (iota((128, 256), 1) >> 4)
+        row_k = iota((16, 256), 0)
+        rows = pl.ds(pl.multiple_of(64 * (entry >> 4), 64), 128)
+        zmodes = column_cells(rows, rh, rl, sel[m], lzh[...], lzl[...], same)
+        dense = jnp.zeros((16, 256), f32)
+        for k in range(16):
+            single = jnp.where(row_k == k, zmodes, 0.0).astype(bf16)
+            dense = dense + dot_t(single, inv[k])
+        dh, dl = split(dense)
+        back = dot3(lzth[...], lztl[...], dh, dl)
+        gh, gl = split(jnp.where(same, back, 0.0))
+        cut[rows, :] += dot(gh, sel_t[m]) + dot(gl, sel_t[m])
+
+
+def is_late_row():
+    return lax.axis_index("gx") == lax.axis_size("gx") // 2
+
+
+def inner_work(
+    sw, lw, aw, yh, yl, lh, ll, ayh, ayl, khl, kth, ktl, dinv, listed, inverse,
+    syh, syl, rh, rl, ryh, ryl, tin, inv, sem,
 ):
-    listed = pltpu.make_async_copy(cols_hbm, cols, sem.at[2])
-    listed.start()
-    copies = [pltpu.make_async_copy(inverse.at[m], inv.at[m], sem.at[m]) for m in range(2)]
-    for copy in copies:
-        copy.start()
+    bulk = pltpu.make_async_copy(inverse.at[1], inv, sem)
+    bulk.start()
     sh, sl = split(sw[...])
     syh[...], syl[...] = split(dot3(sh, sl, yh[...], yl[...]))
     spread = jnp.where((iota((192, 32), 0) >> 3) + 4 == iota((192, 32), 1), 1.0, 0.0)
     live = dot(spread.astype(bf16), aw[...].astype(bf16))
+    rh[0:64, :] = jnp.zeros((64, 256), bf16)
+    rl[0:64, :] = jnp.zeros((64, 256), bf16)
+    rh[256:320, :] = jnp.zeros((64, 256), bf16)
+    rl[256:320, :] = jnp.zeros((64, 256), bf16)
     for o in range(3):
         rows, mine = slice(64 * o, 64 * o + 128), slice(64 * o, 64 * o + 64)
         load = lw[64 * o + 32 : 64 * o + 96, :]
-        rh[mine, :], rl[mine, :] = stencil(
+        into = slice(64 * o + 64, 64 * o + 128)
+        rh[into, :], rl[into, :] = stencil(
             lh[...], ll[...], syh[rows, :], syl[rows, :], live[mine], load
         )
-    ryh[...], ryl[...] = split(dot3(rh[...], rl[...], ayh[...], ayl[...]))
-    listed.wait()
-    rest = (khl[...], kth[...], ktl[...], dinv[...], cols)
+    ryh[...], ryl[...] = split(dot3(rh[64:256, :], rl[64:256, :], ayh[...], ayl[...]))
+    rest = (khl[...], kth[...], ktl[...], dinv[...], listed[...])
     one = solve_row(1, *rest, ryh[0:128, :], ryl[0:128, :])
     two = solve_row(2, *rest, ryh[64:192, :], ryl[64:192, :])
     tin[0:64, :] = one[0:64]
     tin[64:128, :] = one[64:128] + two[0:64]
     tin[128:192, :] = two[64:128]
-    for copy in copies:
-        copy.wait()
+    bulk.wait()
+
+
+def inner_early_kernel(*refs):
+    held, send, args, outs, sem = refs[15], refs[24], refs[:15], refs[16:24], refs[25]
+    send[...] = held[...]
+
+    @pl.when(is_late_row())
+    def _():
+        inner_work(*args, *outs, sem)
+
+
+def inner_kernel(*refs):
+    args, outs, sem = refs[:15], refs[23:31], refs[31]
+
+    @pl.when(jnp.logical_not(is_late_row()))
+    def _():
+        inner_work(*args, *outs, sem)
 
 
 def edge_kernel(
-    cols_hbm, lw, aw, ra, rb, syh, syl, rh_in, rl_in, ryh, ryl, inv,
+    cols_hbm, lw, aw, ra, rb, syh, syl, rh_in, rl_in, ryh, ryl, inv0, inv1, listed,
     yh, yl, lh, ll, ayh, ayl, ath, atl, khl, kth, ktl, dinv, sel, sel_t, lzh, lzl, lzth, lztl,
     first, last, cut, send_a, send_b, rh, rl, cols, sem,
 ):
-    listed = pltpu.make_async_copy(cols_hbm, cols, sem)
-    listed.start()
+    fetch_cols = pltpu.make_async_copy(cols_hbm, cols, sem)
+    fetch_cols.start()
     px = parity("gx")
     low, high = either(px, rb[...], ra[...]), either(px, ra[...], rb[...])
 
@@ -198,7 +243,7 @@
     sh, sl = split(jnp.concatenate([low[0:64], high[0:64]], axis=0))
     ehh, ehl = split(dot3(sh, sl, yh[...], yl[...]))
     spread = jnp.where((iota((64, 16), 0) >> 3) + 4 == iota((64, 16), 1), 1.0, 0.0).astype(bf16)
-    rh[64:256, :], rl[64:256, :] = rh_in[...], rl_in[...]
+    rh[64:256, :], rl[64:256, :] = rh_in[64:256, :], rl_in[64:256, :]
     live = dot(spread, jnp.concatenate([low[96:104], aw[0:8, :]], axis=0).astype(bf16))
     rh[0:64, :], rl[0:64, :] = stencil(
         lh[...],
@@ -217,28 +262,11 @@
         live,
         jnp.concatenate([lw[224:256, :], high[64:96]], axis=0),
     )
-    same = (iota((128, 256), 0) >> 3) == (iota((128, 256), 1) >> 4)
-    row_k = iota((16, 256), 0)
-    listed.wait()
     cut[...] = jnp.zeros((320, 256), f32)
-    for m in range(2):
-        at = pl.multiple_of(64 * (jnp.maximum(cols[m], 0) >> 4), 64)
-        rows = pl.ds(at, 128)
-        cells = dot(rh[rows, :], sel[m]) + dot(rl[rows, :], sel[m])
-        ch, cl = split(jnp.where(same, cells, 0.0))
-        zmodes = dot3(lzh[...], lzl[...], ch, cl)
-        dense = jnp.zeros((16, 256), f32)
-        for k in range(16):
-            single = jnp.where(row_k == k, zmodes, 0.0).astype(bf16)
-            dense = dense + dot_t(single, inv[m, k])
-        dh, dl = split(dense)
-        back = dot3(lzth[...], lztl[...], dh, dl)
-        gh, gl = split(jnp.where(same, back, 0.0))
-        cut[rows, :] += dot(gh, sel_t[m]) + dot(gl, sel_t[m])
     edges_h = jnp.concatenate([rh[0:64, :], rh[256:320, :]], axis=0)
     edges_l = jnp.concatenate([rl[0:64, :], rl[256:320, :]], axis=0)
     eyh, eyl = split(dot3(edges_h, edges_l, ayh[...], ayl[...]))
-    rest = (khl[...], kth[...], ktl[...], dinv[...], cols)
+    rest = (khl[...], kth[...], ktl[...], dinv[...], listed[...])
     t0 = solve_row(
         0,
         *rest,
@@ -254,6 +282,11 @@
     first[...], last[...] = t0[32:128], t3[0:96]
     th, tl = split(jnp.concatenate([t0[0:32], t3[96:128]], axis=0))
     out = dot3(th, tl, ath[...], atl[...])
+    fetch_cols.wait()
+    for m, inv in enumerate((inv0, inv1)):
+        a = cols[m] >> 4
+        outer = (a == 0) | (a == 3)
+        cut_column(m, outer, cols[m], rh, rl, sel, sel_t, lzh, lzl, lzth, lztl, inv, cut)
     out_low, out_high = out[0:32] + cut[0:32, :], out[32:64] + cut[288:320, :]
     pad = jnp.zeros((96, 128), f32)
     corner_low = jnp.concatenate([pad, out_low[:, 128:256]], axis=0).T
@@ -264,7 +297,13 @@
     send_b[...] = either(px, out_low, out_high)
 
 
-def spread_kernel(first, last, tin, cut, ath, atl, core, side):
+def spread_kernel(
+    cols_hbm, first, last, tin, cut_in, ath, atl, rh, rl, inv0, inv1,
+    sel, sel_t, lzh, lzl, lzth, lztl, core, side, cut, cols, sem,
+):
+    fetch_cols = pltpu.make_async_copy(cols_hbm, cols, sem)
+    fetch_cols.start()
+    cut[...] = cut_in[...]
     total = jnp.concatenate(
         [
             first[0:32, :],
@@ -276,7 +315,13 @@
         axis=0,
     )
     th, tl = split(total)
-    total = dot3(th, tl, ath[...], atl[...]) + cut[32:288, :]
+    total = dot3(th, tl, ath[...], atl[...])
+    fetch_cols.wait()
+    for m, inv in enumerate((inv0, inv1)):
+        a = cols[m] >> 4
+        middle = (a == 1) | (a == 2)
+        cut_column(m, middle, cols[m], rh, rl, sel, sel_t, lzh, lzl, lzth, lztl, inv, cut)
+    total = total + cut[32:288, :]
     core[...] = total[:, 0:128]
     side[...] = total[:, 128:256].T[0:16]
 
@@ -306,11 +351,13 @@
 
 
 def build_kernel(
-    after, stiff_hbm, mass_hbm, basis_hbm, values_hbm, cols_hbm,
-    yh, yl, lh, ll, ayh, ayl, ath, atl, khl, kth, ktl, dinv, sel, sel_t, lzh, lzl, lzth, lztl,
+    after, stiff_hbm, mass_hbm, basis_hbm, values_hbm, cols_hbm, inverse,
+    yh, yl, lh, ll, ayh, ayl, ath, atl, khl, kth, ktl, dinv, sel, sel_t, lzh, lzl, lzth, lztl, inv, listed,
     stiff, mass, basis, values, cols, sem,
 ):
     del after
+    bulk = pltpu.make_async_copy(inverse.at[0], inv, sem.at[5])
+    bulk.start()
     fetch(
         [
             (stiff_hbm, stiff),
@@ -372,9 +419,11 @@
         at = jnp.where(entry >= 0, 8 * (jnp.maximum(entry, 0) & 15) - 4, -4 * FAR)
         sel[m] = one(cy == yy + at)
         sel_t[m] = one(cy_t == yy_t + at)
-
-
-def call(kernel, outs, ins, scratch=(), name=None, flops=10**6, limit=8 * 2**20):
+        listed[8 * m : 8 * m + 8, :] = jnp.full((8, 128), entry, jnp.int32)
+    bulk.wait()
+
+
+def call(kernel, outs, ins, scratch=(), name=None, aliases=None, limit=8 * 2**20):
     return pl.pallas_call(
         kernel,
         out_shape=[jax.ShapeDtypeStruct(s, t) for s, t in outs],
@@ -383,7 +432,8 @@
         scratch_shapes=scratch,
         name=name,
         compiler_params=pltpu.CompilerParams(vmem_limit_bytes=limit),
-        cost_estimate=pl.CostEstimate(flops=flops, bytes_accessed=10**6, transcendentals=0),
+        input_output_aliases=aliases or {},
+        cost_estimate=pl.CostEstimate(flops=10**6, bytes_accessed=10**6, transcendentals=0),
     )
 
 
@@ -431,7 +481,7 @@
     )(st, ld, active)
     ya, yb = exchange(ya, yb, "gy")
     sq = ((256, 256), bf16)
-    yh, yl, lh, ll, ayh, ayl, ath, atl, khl, kth, ktl, dinv, *cutters = call(
+    *mats, inv0, listed = call(
         build_kernel,
         [
             ((256, 512), bf16), ((256, 512), bf16), ((64, 256), bf16), ((64, 256), bf16),
@@ -439,45 +489,55 @@
             sq, ((128, 256), bf16), ((128, 256), bf16),
             ((256, 256), f32), ((2, 256, 256), bf16), ((2, 256, 256), bf16),
             ((16, 128), bf16), ((16, 128), bf16), ((128, 16), bf16), ((128, 16), bf16),
-        ],
-        [VMEM] + [ANY] * 5,
+            ((PATCH, 256, 256), bf16), ((16, 128), jnp.int32),
+        ],
+        [VMEM] + [ANY] * 6,
         [
             pltpu.SMEM((3, 5), f32),
             pltpu.SMEM((3, 5), f32),
             pltpu.VMEM((3, 16, 16), f32),
             pltpu.VMEM((3, 16), f32),
             pltpu.SMEM((2,), jnp.int32),
-            dma((5,)),
+            dma((6,)),
         ],
         name="build",
-        limit=8 * 2**20,
-    )(ac, stiff, mass, basis, values, cols_in)
+    )(ac, stiff, mass, basis, values, cols_in, inverse)
+    yh, yl, lh, ll, ayh, ayl, ath, atl, khl, kth, ktl, dinv, *cutters = mats
     sw, lw, aw, xa, xb = call(
         pack_x_kernel,
         [((256, 256), f32), ((256, 256), f32), ((32, 256), f32), ((120, 128), f32), ((120, 128), f32)],
         [VMEM] * 6,
         name="pack_x",
     )(lh, s, l, ac, ya, yb)
+    inner_outs = [
+        ((256, 512), bf16), ((256, 512), bf16),
+        ((320, 256), bf16), ((320, 256), bf16), ((192, 256), bf16), ((192, 256), bf16),
+        ((192, 256), f32), ((PATCH, 256, 256), bf16),
+    ]
+    inner_args = (sw, lw, aw, yh, yl, lh, ll, ayh, ayl, khl, kth, ktl, dinv, listed, inverse)
+    *early, xb = call(
+        inner_early_kernel,
+        inner_outs + [((120, 128), f32)],
+        [VMEM] * 14 + [ANY, VMEM],
+        [dma],
+        name="inner_early",
+    )(*inner_args, xb)
     xa, xb = exchange(xa, xb, "gx")
-    syh, syl, rh, rl, ryh, ryl, tin, inv = call(
+    syh, syl, rh, rl, ryh, ryl, tin, inv1 = call(
         inner_kernel,
-        [
-            ((256, 512), bf16), ((256, 512), bf16),
-            ((192, 256), bf16), ((192, 256), bf16), ((192, 256), bf16), ((192, 256), bf16),
-            ((192, 256), f32), ((2, PATCH, 256, 256), bf16),
-        ],
-        [ANY] + [VMEM] * 13 + [ANY],
-        [pltpu.SMEM((2,), jnp.int32), dma((3,))],
+        inner_outs,
+        [VMEM] * 14 + [ANY] + [VMEM] * 8,
+        [dma],
         name="inner",
-        limit=12 * 2**20,
-    )(cols_in, sw, lw, aw, yh, yl, lh, ll, ayh, ayl, khl, kth, ktl, dinv, inverse)
+        aliases={15 + n: n for n in range(8)},
+    )(*inner_args, *early)
     first, last, cut, xa, xb = call(
         edge_kernel,
         [
             ((96, 256), f32), ((96, 256), f32), ((320, 256), f32),
             ((48, 128), f32), ((48, 128), f32),
         ],
-        [ANY] + [VMEM] * 29,
+        [ANY] + [VMEM] * 31,
         [
             pltpu.VMEM((320, 256), bf16),
             pltpu.VMEM((320, 256), bf16),
@@ -486,13 +546,17 @@
         ],
         name="edge",
     )(
-        cols_in, lw, aw, xa, xb, syh, syl, rh, rl, ryh, ryl, inv,
+        cols_in, lw, aw, xa, xb, syh, syl, rh, rl, ryh, ryl, inv0, inv1, listed,
         yh, yl, lh, ll, ayh, ayl, ath, atl, khl, kth, ktl, dinv, *cutters,
     )
     xa, xb = exchange(xa, xb, "gx")
     core, side = call(
-        spread_kernel, [((256, 128), f32), ((16, 256), f32)], [VMEM] * 6, name="spread"
-    )(first, last, tin, cut, ath, atl)
+        spread_kernel,
+        [((256, 128), f32), ((16, 256), f32)],
+        [ANY] + [VMEM] * 16,
+        [pltpu.VMEM((320, 256), f32), pltpu.SMEM((2,), jnp.int32), dma],
+        name="spread",
+    )(cols_in, first, last, tin, cut, ath, atl, rh, rl, inv0, inv1, *cutters)
     ya, yb = call(
         join_x_kernel, [((8, 256), f32), ((8, 256), f32)], [VMEM] * 3, name="join_x"
     )(side, xa, xb)

time: 44.2 us -> 42.2 us (0.955)
  Pallas kernels: 12.8 us -> 9.37 us
  waiting for transfers between devices: 7.34 us -> 9.84 us
  starting transfers between devices: 23.7 us -> 22.5 us
    pallas_call x1, Pallas kernels: 5.44 us -> 1.76 us  [on_device(): call(edge_kernel, [((96, 256), f32), ((96, 256), f32), ((320, 256), f32),...]
    ppermute x4, waiting for transfers between devices: 7.33 us -> 9.83 us  [exchange(): lax.ppermute(b, axis, swaps(axis, 1))]
    ppermute x4, starting transfers between devices: 21.5 us -> 20.3 us  [exchange(): lax.ppermute(b, axis, swaps(axis, 1))]
    pallas_call x1, Pallas kernels: 1.94 us -> 2.49 us  [on_device(): call(build_kernel, [((256, 512), bf16), ((256, 512), bf16), ((64, 256), b...]
    pallas_call x2 -> x3, Pallas kernels: 3.24 us -> 2.91 us  [the longest x1 2.08 us: on_device(): call(inner_early_kernel, inner_outs + [((120, 128), f32)], [VMEM] * 14 +...]
  transfers between devices with their start and end apart: 8 -> 8, of which waited for: 3 -> 3; matrix products, arithmetic and copies ran while one was open for 0% -> 0% of each run, Pallas kernels for 12% -> 13%
where the time goes in v3:
time: 42.2 us; the launch traced here: 41.9 us
  starting transfers between devices  22.5 us (53%)
  waiting for transfers between devices  9.84 us (23%)
  Pallas kernels  9.37 us (22%)
    ppermute x4, starting transfers between devices, exchange(): lax.ppermute(b, axis, swaps(axis, 1))  20.3 us
    ppermute x4, waiting for transfers between devices, exchange(): lax.ppermute(b, axis, swaps(axis, 1))  9.83 us
    pallas_call x1, Pallas kernels, on_device(): call(build_kernel, [((256, 512), bf16), ((256, 512), bf16), ((64, 256), b...  2.49 us
    ppermute x4, starting transfers between devices, exchange(): lax.ppermute(a, axis, swaps(axis, 0))  2.16 us
    pallas_call x1, Pallas kernels, on_device(): call(inner_early_kernel, inner_outs + [((120, 128), f32)], [VMEM] * 14 +...  2.08 us
    pallas_call x1, Pallas kernels, on_device(): call(edge_kernel, [((96, 256), f32), ((96, 256), f32), ((320, 256), f32),...  1.76 us
    pallas_call x1, Pallas kernels, on_device(): call(pack_y_kernel, [((256, 128), f32), ((256, 128), f32), ((32, 128), f3...  1.2 us
  transfers between devices with their start and end apart: 8, of which 3 were waited for; matrix products, arithmetic and copies ran while one was open for 0% of the time, Pallas kernels for 13%

profile of v3, /device:TPU:24, one launch (start us, length us, event | category | flops | bytes accessed | tf_op | source)
XLA Modules:
  0.0 41.9 jit_solution(11212482770053449814)
XLA Ops:
  0.0 1.2 %pack_y.1 = (f32[256,128]{1,0:T(8,128)S(1)}, f32[256,128]{1,0:T(8,128)S(1)}, f32[32,128]{1,0:T(8,128)S(1)}, f32[8,640]{1,0:T(8,128)S(1)}, f32[8,640]{1,0:T(8,128)S(1)}) custom-call(f32[256,128]{1,0:T(8,128)} %bitcast.8, bf16[256,128]{1,0:T(8,128)(2,1)} %bitcast.9, s32[32,128]{1,0:T(8,128)} %ac_hbm.1), custom_call_target="tpu_custom_call" | custom-call | flops 1000000 | bytes 1000000 | tf_op jit(solution)/shard_map/pack_y/pallas_call | solution.py:468
  1.2 0.1 collective-permute-start
  1.3 4.9 %collective-permute-start.1 = (f32[8,640]{1,0:T(8,128)S(1)}, f32[8,640]{1,0:T(8,128)S(1)}, u32[]{:S(2)}, u32[]{:S(2)}) collective-permute-start(f32[8,640]{1,0:T(8,128)S(1)} %get-tuple-element.66), channel_id=1, source_target_pairs={{1,2},{3,4},{5,6},{7,8},{9,10},{11,12},{13,14},{2,1},{4,3},{6,5},{... | collective-permute-start | bytes 61448 | tf_op jit(solution)/shard_map/ppermute | solution.py:447
  6.2 2.5 %build.1 = (bf16[256,512]{1,0:T(8,128)(2,1)S(1)}, bf16[256,512]{1,0:T(8,128)(2,1)S(1)}, bf16[64,256]{1,0:T(8,128)(2,1)S(1)}, bf16[64,256]{1,0:T(8,128)(2,1)S(1)}...) custom-call(f32[32,128]{1,0:T(8,128)S(1)} %get-tuple-element.61.afte, ...), custom_call_target="tpu_custom_call" | custom-call | flops 1000000 | bytes 1000000 | tf_op jit(solution)/shard_map/build/pallas_call | solution.py:484
  8.7 0.0 collective-permute-done.ra
  8.8 0.0 collective-permute-done.1.rb
  8.8 0.2 pack_x.1
  8.9 2.0 %collective-permute-start.2 = (f32[120,128]{1,0:T(8,128)S(1)}, f32[120,128]{1,0:T(8,128)S(1)}, u32[]{:S(2)}, u32[]{:S(2)}) collective-permute-start(f32[120,128]{1,0:T(8,128)S(1)} %get-tuple-element.69), channel_id=1, source_target_pairs={{0,16},{32,48},{64,80},{96,112},{128,144},{160,176},{192,208},{224... | collective-permute-start | bytes 184328 | tf_op jit(solution)/shard_map/ppermute | solution.py:447
  10.9 2.1 %inner_early.1 = (bf16[256,512]{1,0:T(8,128)(2,1)S(1)}, bf16[256,512]{1,0:T(8,128)(2,1)S(1)}, bf16[320,256]{1,0:T(8,128)(2,1)S(1)}, bf16[320,256]{1,0:T(8,128)(2...) custom-call(f32[256,256]{1,0:T(8,128)S(1)} %get-tuple-element.70.ref, ...), custom_call_target="tpu_custom_call" | custom-call | flops 1000000 | bytes 1000000 | tf_op jit(solution)/shard_map/inner_early/pallas_call | solution.py:518
  13.0 5.2 %collective-permute-start.3 = (f32[120,128]{1,0:T(8,128)S(1)}, f32[120,128]{1,0:T(8,128)S(1)}, u32[]{:S(2)}, u32[]{:S(2)}) collective-permute-start(f32[120,128]{1,0:T(8,128)S(1)} %get-tuple-element.82), channel_id=1, source_target_pairs={{16,32},{48,64},{80,96},{112,128},{144,160},{176,192},{208,224},{3... | collective-permute-start | bytes 184328 | tf_op jit(solution)/shard_map/ppermute | solution.py:447
  18.2 0.1 inner.1
  18.3 0.0 collective-permute-done.2.ra
  18.3 4.4 %collective-permute-done.3.rb = f32[120,128]{1,0:T(8,128)S(1)} collective-permute-done((f32[120,128]{1,0:T(8,128)S(1)}, f32[120,128]{1,0:T(8,128)S(1)}, u32[]{:S(2)}, u32[]{:S(2)}) %collective-permute-start.3) | collective-permute-done | bytes 61472 | tf_op jit(solution)/shard_map/ppermute | solution.py:447
  22.7 1.8 %edge.1 = (f32[96,256]{1,0:T(8,128)S(1)}, f32[96,256]{1,0:T(8,128)S(1)}, f32[320,256]{1,0:T(8,128)S(1)}, f32[48,128]{1,0:T(8,128)S(1)}, f32[48,128]{1,0:T(8,128)S(1)}) custom-call(s32[2]{0:T(128)} %bitcast.11, f32[256,256]{1,0:T(8,128)S(1)} %get-tuple-element.67.refs_1_.lw, f32[32,256]{1,0:T(8,128)S(1)} %get-tuple-element.68.refs_2_.aw, ...), custom_call_target="tpu_custom_call" | custom-call | flops 1000000 | bytes 1000000 | tf_op jit(solution)/shard_map/edge/pallas_call | solution.py:534
  24.5 0.1 collective-permute-start.4
  24.6 6.7 %collective-permute-start.5 = (f32[48,128]{1,0:T(8,128)S(1)}, f32[48,128]{1,0:T(8,128)S(1)}, u32[]{:S(2)}, u32[]{:S(2)}) collective-permute-start(f32[48,128]{1,0:T(8,128)S(1)} %get-tuple-element.113), channel_id=1, source_target_pairs={{16,32},{48,64},{80,96},{112,128},{144,160},{176,192},{208,224},{3... | collective-permute-start | bytes 73736 | tf_op jit(solution)/shard_map/ppermute | solution.py:447
  31.3 0.8 %spread.1 = (f32[256,128]{1,0:T(8,128)S(1)}, f32[16,256]{1,0:T(8,128)S(1)}) custom-call(s32[2]{0:T(128)} %bitcast.12, f32[96,256]{1,0:T(8,128)S(1)} %get-tuple-element.107.first, f32[96,256]{1,0:T(8,128)S(1)} %get-tuple-element.108.last, f32[192,256]{1,0:T(8,128)S(1)} %get-tuple-element.109.tin, f32[320,256]{1,0:T(8,128)S(1)} %get-tuple-element.110.cut_in, ...), custom_call_target="tpu_custom_call" | custom-call | flops 1000000 | bytes 1000000 | tf_op jit(solution)/shard_map/spread/pallas_call | solution.py:553
  32.1 0.0 collective-permute-done.4.ra.xa
  32.1 1.9 %collective-permute-done.5.rb.xb = f32[48,128]{1,0:T(8,128)S(1)} collective-permute-done((f32[48,128]{1,0:T(8,128)S(1)}, f32[48,128]{1,0:T(8,128)S(1)}, u32[]{:S(2)}, u32[]{:S(2)}) %collective-permute-start.5) | collective-permute-done | bytes 24608 | tf_op jit(solution)/shard_map/ppermute | solution.py:447
  34.0 0.0 collective-permute-start.6
  34.0 3.5 %collective-permute-start.7 = (f32[8,256]{1,0:T(8,128)S(1)}, f32[8,256]{1,0:T(8,128)S(1)}, u32[]{:S(2)}, u32[]{:S(2)}) collective-permute-start(f32[8,256]{1,0:T(8,128)S(1)} %get-tuple-element.116), channel_id=1, source_target_pairs={{1,2},{3,4},{5,6},{7,8},{9,10},{11,12},{13,14},{2,1},{4,3},{6,5},{... | collective-permute-start | bytes 24584 | tf_op jit(solution)/shard_map/ppermute | solution.py:447
  37.5 0.0 collective-permute-done.6.ya
  37.5 3.5 %collective-permute-done.7.yb = f32[8,256]{1,0:T(8,128)S(1)} collective-permute-done((f32[8,256]{1,0:T(8,128)S(1)}, f32[8,256]{1,0:T(8,128)S(1)}, u32[]{:S(2)}, u32[]{:S(2)}) %collective-permute-start.7) | collective-permute-done | bytes 8224 | tf_op jit(solution)/shard_map/ppermute | solution.py:447
  41.0 0.8 %finish.1 = f32[256,128]{1,0:T(8,128)} custom-call(f32[256,128]{1,0:T(8,128)S(1)} %get-tuple-element.111.core, f32[48,128]{1,0:T(8,128)S(1)} %collective-permute-done.4.ra.xa, f32[48,128]{1,0:T(8,128)S(1)} %collective-permute-done.5.rb.xb, f32[8,256]{1,0:T(8,128)S(1)} %collective-permute-done.6.ya, f32[8,256]{1,0:T(8,128)S(1)} %collective-permute-done.7.yb, ...), custom_call_target="tpu_custom_call" | custom-call | flops 1000000 | bytes 1000000 | tf_op jit(solution)/shard_map/finish/pallas_call | solution.py:564
  (1 shorter events, 0.0 us)
Async XLA Ops:
  1.2 7.5 %collective-permute-start = (f32[8,640]{1,0:T(8,128)S(1)}, f32[8,640]{1,0:T(8,128)S(1)}, u32[]{:S(2)}, u32[]{:S(2)}) collective-permute-start(f32[8,640]{1,0:T(8,128)S(1)} %get-tuple-element.65), channel_id=1, source_target_pairs={{0,1},{2,3},{4,5},{6,7},{8,9},{10,11},{12,13},{14,15},{1,0},{3,2},... | collective-permute-start | bytes 61448 | tf_op jit(solution)/shard_map/ppermute | solution.py:447
  1.3 7.5 %collective-permute-start.1 = (f32[8,640]{1,0:T(8,128)S(1)}, f32[8,640]{1,0:T(8,128)S(1)}, u32[]{:S(2)}, u32[]{:S(2)}) collective-permute-start(f32[8,640]{1,0:T(8,128)S(1)} %get-tuple-element.66), channel_id=1, source_target_pairs={{1,2},{3,4},{5,6},{7,8},{9,10},{11,12},{13,14},{2,1},{4,3},{6,5},{... | collective-permute-start | bytes 61448 | tf_op jit(solution)/shard_map/ppermute | solution.py:447
  8.9 9.3 %collective-permute-start.2 = (f32[120,128]{1,0:T(8,128)S(1)}, f32[120,128]{1,0:T(8,128)S(1)}, u32[]{:S(2)}, u32[]{:S(2)}) collective-permute-start(f32[120,128]{1,0:T(8,128)S(1)} %get-tuple-element.69), channel_id=1, source_target_pairs={{0,16},{32,48},{64,80},{96,112},{128,144},{160,176},{192,208},{224... | collective-permute-start | bytes 184328 | tf_op jit(solution)/shard_map/ppermute | solution.py:447
  13.0 9.7 %collective-permute-start.3 = (f32[120,128]{1,0:T(8,128)S(1)}, f32[120,128]{1,0:T(8,128)S(1)}, u32[]{:S(2)}, u32[]{:S(2)}) collective-permute-start(f32[120,128]{1,0:T(8,128)S(1)} %get-tuple-element.82), channel_id=1, source_target_pairs={{16,32},{48,64},{80,96},{112,128},{144,160},{176,192},{208,224},{3... | collective-permute-start | bytes 184328 | tf_op jit(solution)/shard_map/ppermute | solution.py:447
  24.5 7.5 %collective-permute-start.4 = (f32[48,128]{1,0:T(8,128)S(1)}, f32[48,128]{1,0:T(8,128)S(1)}, u32[]{:S(2)}, u32[]{:S(2)}) collective-permute-start(f32[48,128]{1,0:T(8,128)S(1)} %get-tuple-element.112), channel_id=1, source_target_pairs={{0,16},{32,48},{64,80},{96,112},{128,144},{160,176},{192,208},{224... | collective-permute-start | bytes 73736 | tf_op jit(solution)/shard_map/ppermute | solution.py:447
  24.6 9.3 %collective-permute-start.5 = (f32[48,128]{1,0:T(8,128)S(1)}, f32[48,128]{1,0:T(8,128)S(1)}, u32[]{:S(2)}, u32[]{:S(2)}) collective-permute-start(f32[48,128]{1,0:T(8,128)S(1)} %get-tuple-element.113), channel_id=1, source_target_pairs={{16,32},{48,64},{80,96},{112,128},{144,160},{176,192},{208,224},{3... | collective-permute-start | bytes 73736 | tf_op jit(solution)/shard_map/ppermute | solution.py:447
  34.0 3.6 %collective-permute-start.6 = (f32[8,256]{1,0:T(8,128)S(1)}, f32[8,256]{1,0:T(8,128)S(1)}, u32[]{:S(2)}, u32[]{:S(2)}) collective-permute-start(f32[8,256]{1,0:T(8,128)S(1)} %get-tuple-element.115), channel_id=1, source_target_pairs={{0,1},{2,3},{4,5},{6,7},{8,9},{10,11},{12,13},{14,15},{1,0},{3,2},... | collective-permute-start | bytes 24584 | tf_op jit(solution)/shard_map/ppermute | solution.py:447
  34.0 7.1 %collective-permute-start.7 = (f32[8,256]{1,0:T(8,128)S(1)}, f32[8,256]{1,0:T(8,128)S(1)}, u32[]{:S(2)}, u32[]{:S(2)}) collective-permute-start(f32[8,256]{1,0:T(8,128)S(1)} %get-tuple-element.116), channel_id=1, source_target_pairs={{1,2},{3,4},{5,6},{7,8},{9,10},{11,12},{13,14},{2,1},{4,3},{6,5},{... | collective-permute-start | bytes 24584 | tf_op jit(solution)/shard_map/ppermute | solution.py:447

commit v4 on v3

--- a/solution.py
+++ b/solution.py
@@ -1,5 +1,3 @@
-import functools
-
 import jax
 import jax.numpy as jnp
 from jax import lax
@@ -107,8 +105,10 @@
     send_b[...] = either(py, low, high)
 
 
-def pack_x_kernel(after, s, l, ac, ra, rb, sw, lw, aw, send_a, send_b):
+def pack_x_kernel(after, s, l, ac, *refs):
     del after
+    ra, rb = refs[0], refs[1]
+    sw, lw, aw, send_a, send_b = refs[-5:]
     px = parity("gx")
 
     def strips(lanes, width):
@@ -150,34 +150,43 @@
     return dot3(kth, ktl, mh, ml)
 
 
-def column_cells(rows, rh, rl, sel, lzh, lzl, same):
-    cells = dot(rh[rows, :], sel) + dot(rl[rows, :], sel)
-    ch, cl = split(jnp.where(same, cells, 0.0))
-    return dot3(lzh, lzl, ch, cl)
-
-
-def cut_column(m, here, entry, rh, rl, sel, sel_t, lzh, lzl, lzth, lztl, inv, cut):
-    @pl.when((entry >= 0) & here)
-    def _():
-        same = (iota((128, 256), 0) >> 3) == (iota((128, 256), 1) >> 4)
-        row_k = iota((16, 256), 0)
-        rows = pl.ds(pl.multiple_of(64 * (entry >> 4), 64), 128)
-        zmodes = column_cells(rows, rh, rl, sel[m], lzh[...], lzl[...], same)
-        dense = jnp.zeros((16, 256), f32)
-        for k in range(16):
-            single = jnp.where(row_k == k, zmodes, 0.0).astype(bf16)
-            dense = dense + dot_t(single, inv[k])
-        dh, dl = split(dense)
-        back = dot3(lzth[...], lztl[...], dh, dl)
+def cut_values(ms, cols, rh, rl, sel, sel_t, lzh, lzl, lzth, lztl, invs):
+    same = (iota((128, 256), 0) >> 3) == (iota((128, 256), 1) >> 4)
+    lane_k = iota((256, 16), 1)
+    rows = [pl.ds(pl.multiple_of(64 * (cols[m] >> 4), 64), 128) for m in ms]
+    cells = [dot(rh[r, :], sel[m]) + dot(rl[r, :], sel[m]) for m, r in zip(ms, rows)]
+    cells = [split(jnp.where(same, c, 0.0)) for c in cells]
+    zmodes = [dot3(lzh[...], lzl[...], ch, cl).astype(bf16) for ch, cl in cells]
+    wide = [z.astype(f32) for z in zmodes]
+    dense = [jnp.zeros((256, 16), f32) for m in ms]
+    for k in range(16):
+        for n, m in enumerate(ms):
+            if k % 2:
+                terms = invs[m][k].astype(f32) * wide[n][k : k + 1]
+                column = jnp.sum(terms, axis=1, keepdims=True)
+            else:
+                column = dot_t(invs[m][k], zmodes[n])
+            dense[n] = jnp.where(lane_k == k, column, dense[n])
+    out = []
+    for m, r, d in zip(ms, rows, dense):
+        dh, dl = split(d)
+        back = dot_t(lzth[...], dh) + (dot_t(lzth[...], dl) + dot_t(lztl[...], dh))
         gh, gl = split(jnp.where(same, back, 0.0))
-        cut[rows, :] += dot(gh, sel_t[m]) + dot(gl, sel_t[m])
-
-
-def is_late_row():
-    return lax.axis_index("gx") == lax.axis_size("gx") // 2
-
-
-def inner_work(
+        out.append((r, dot(gh, sel_t[m]) + dot(gl, sel_t[m])))
+    return out
+
+
+def by_case(cols, places, body):
+    need = []
+    for m in range(2):
+        a = cols[m] >> 4
+        need.append((a == places[0]) | (a == places[1]))
+    for ms in ((), (0,), (1,), (0, 1)):
+        wanted = [need[m] if m in ms else jnp.logical_not(need[m]) for m in range(2)]
+        pl.when(wanted[0] & wanted[1])(lambda ms=ms: body(ms))
+
+
+def inner_kernel(
     sw, lw, aw, yh, yl, lh, ll, ayh, ayl, khl, kth, ktl, dinv, listed, inverse,
     syh, syl, rh, rl, ryh, ryl, tin, inv, sem,
 ):
@@ -208,32 +217,16 @@
     bulk.wait()
 
 
-def inner_early_kernel(*refs):
-    held, send, args, outs, sem = refs[15], refs[24], refs[:15], refs[16:24], refs[25]
-    send[...] = held[...]
-
-    @pl.when(is_late_row())
-    def _():
-        inner_work(*args, *outs, sem)
-
-
-def inner_kernel(*refs):
-    args, outs, sem = refs[:15], refs[23:31], refs[31]
-
-    @pl.when(jnp.logical_not(is_late_row()))
-    def _():
-        inner_work(*args, *outs, sem)
-
-
 def edge_kernel(
-    cols_hbm, lw, aw, ra, rb, syh, syl, rh_in, rl_in, ryh, ryl, inv0, inv1, listed,
+    lw, aw, syh, syl, rh_in, rl_in, ryh, ryl, inv0, inv1, listed,
     yh, yl, lh, ll, ayh, ayl, ath, atl, khl, kth, ktl, dinv, sel, sel_t, lzh, lzl, lzth, lztl,
-    first, last, cut, send_a, send_b, rh, rl, cols, sem,
+    *refs,
 ):
-    fetch_cols = pltpu.make_async_copy(cols_hbm, cols, sem)
-    fetch_cols.start()
+    ra, rb = refs[0][...], refs[1][...]
+    first, last, cut, send_a, send_b, rh, rl = refs[-7:]
+    cols = [listed[8 * m, 0] for m in range(2)]
     px = parity("gx")
-    low, high = either(px, rb[...], ra[...]), either(px, ra[...], rb[...])
+    low, high = either(px, rb, ra), either(px, ra, rb)
 
     def halo(block):
         corner = jnp.concatenate([block[104:120], jnp.zeros((112, 128), f32)], axis=0).T
@@ -263,78 +256,85 @@
         jnp.concatenate([lw[224:256, :], high[64:96]], axis=0),
     )
     cut[...] = jnp.zeros((320, 256), f32)
-    edges_h = jnp.concatenate([rh[0:64, :], rh[256:320, :]], axis=0)
-    edges_l = jnp.concatenate([rl[0:64, :], rl[256:320, :]], axis=0)
-    eyh, eyl = split(dot3(edges_h, edges_l, ayh[...], ayl[...]))
-    rest = (khl[...], kth[...], ktl[...], dinv[...], listed[...])
-    t0 = solve_row(
-        0,
-        *rest,
-        jnp.concatenate([eyh[0:64], ryh[0:64, :]], axis=0),
-        jnp.concatenate([eyl[0:64], ryl[0:64, :]], axis=0),
-    )
-    t3 = solve_row(
-        3,
-        *rest,
-        jnp.concatenate([ryh[128:192, :], eyh[64:128]], axis=0),
-        jnp.concatenate([ryl[128:192, :], eyl[64:128]], axis=0),
-    )
-    first[...], last[...] = t0[32:128], t3[0:96]
-    th, tl = split(jnp.concatenate([t0[0:32], t3[96:128]], axis=0))
-    out = dot3(th, tl, ath[...], atl[...])
-    fetch_cols.wait()
-    for m, inv in enumerate((inv0, inv1)):
-        a = cols[m] >> 4
-        outer = (a == 0) | (a == 3)
-        cut_column(m, outer, cols[m], rh, rl, sel, sel_t, lzh, lzl, lzth, lztl, inv, cut)
-    out_low, out_high = out[0:32] + cut[0:32, :], out[32:64] + cut[288:320, :]
-    pad = jnp.zeros((96, 128), f32)
-    corner_low = jnp.concatenate([pad, out_low[:, 128:256]], axis=0).T
-    corner_high = jnp.concatenate([out_high[:, 128:256], pad], axis=0).T
-    out_low = jnp.concatenate([out_low[:, 0:128], corner_low[0:16]], axis=0)
-    out_high = jnp.concatenate([out_high[:, 0:128], corner_high[0:16]], axis=0)
-    send_a[...] = either(px, out_high, out_low)
-    send_b[...] = either(px, out_low, out_high)
+
+    def tail(ms):
+        args = (rh, rl, sel, sel_t, lzh, lzl, lzth, lztl, (inv0, inv1))
+        values = cut_values(ms, cols, *args)
+        edges_h = jnp.concatenate([rh[0:64, :], rh[256:320, :]], axis=0)
+        edges_l = jnp.concatenate([rl[0:64, :], rl[256:320, :]], axis=0)
+        eyh, eyl = split(dot3(edges_h, edges_l, ayh[...], ayl[...]))
+        rest = (khl[...], kth[...], ktl[...], dinv[...], listed[...])
+        t0 = solve_row(
+            0,
+            *rest,
+            jnp.concatenate([eyh[0:64], ryh[0:64, :]], axis=0),
+            jnp.concatenate([eyl[0:64], ryl[0:64, :]], axis=0),
+        )
+        t3 = solve_row(
+            3,
+            *rest,
+            jnp.concatenate([ryh[128:192, :], eyh[64:128]], axis=0),
+            jnp.concatenate([ryl[128:192, :], eyl[64:128]], axis=0),
+        )
+        first[...], last[...] = t0[32:128], t3[0:96]
+        th, tl = split(jnp.concatenate([t0[0:32], t3[96:128]], axis=0))
+        out = dot3(th, tl, ath[...], atl[...])
+        for rows, value in values:
+            cut[rows, :] += value
+        out_low, out_high = out[0:32] + cut[0:32, :], out[32:64] + cut[288:320, :]
+        pad = jnp.zeros((96, 128), f32)
+        corner_low = jnp.concatenate([pad, out_low[:, 128:256]], axis=0).T
+        corner_high = jnp.concatenate([out_high[:, 128:256], pad], axis=0).T
+        out_low = jnp.concatenate([out_low[:, 0:128], corner_low[0:16]], axis=0)
+        out_high = jnp.concatenate([out_high[:, 0:128], corner_high[0:16]], axis=0)
+        send_a[...] = either(px, out_high, out_low)
+        send_b[...] = either(px, out_low, out_high)
+
+    by_case(cols, (0, 3), tail)
 
 
 def spread_kernel(
-    cols_hbm, first, last, tin, cut_in, ath, atl, rh, rl, inv0, inv1,
-    sel, sel_t, lzh, lzl, lzth, lztl, core, side, cut, cols, sem,
+    listed, first, last, tin, cut_in, ath, atl, rh, rl, inv0, inv1,
+    sel, sel_t, lzh, lzl, lzth, lztl, core, side, cut,
 ):
-    fetch_cols = pltpu.make_async_copy(cols_hbm, cols, sem)
-    fetch_cols.start()
+    cols = [listed[8 * m, 0] for m in range(2)]
     cut[...] = cut_in[...]
-    total = jnp.concatenate(
-        [
-            first[0:32, :],
-            first[32:96, :] + tin[0:64, :],
-            tin[64:128, :],
-            tin[128:192, :] + last[0:64, :],
-            last[64:96, :],
-        ],
-        axis=0,
-    )
-    th, tl = split(total)
-    total = dot3(th, tl, ath[...], atl[...])
-    fetch_cols.wait()
-    for m, inv in enumerate((inv0, inv1)):
-        a = cols[m] >> 4
-        middle = (a == 1) | (a == 2)
-        cut_column(m, middle, cols[m], rh, rl, sel, sel_t, lzh, lzl, lzth, lztl, inv, cut)
-    total = total + cut[32:288, :]
-    core[...] = total[:, 0:128]
-    side[...] = total[:, 128:256].T[0:16]
-
-
-def join_x_kernel(side, ra, rb, send_a, send_b):
+
+    def body(ms):
+        args = (rh, rl, sel, sel_t, lzh, lzl, lzth, lztl, (inv0, inv1))
+        values = cut_values(ms, cols, *args)
+        total = jnp.concatenate(
+            [
+                first[0:32, :],
+                first[32:96, :] + tin[0:64, :],
+                tin[64:128, :],
+                tin[128:192, :] + last[0:64, :],
+                last[64:96, :],
+            ],
+            axis=0,
+        )
+        th, tl = split(total)
+        total = dot3(th, tl, ath[...], atl[...])
+        for rows, value in values:
+            cut[rows, :] += value
+        total = total + cut[32:288, :]
+        core[...] = total[:, 0:128]
+        side[...] = total[:, 128:256].T[0:16]
+
+    by_case(cols, (1, 2), body)
+
+
+def join_x_kernel(side, *refs):
     px = parity("gx")
+    ra, rb = refs[0], refs[1]
+    send_a, send_b = refs[-2:]
     low, high = either(px, rb[32:48, :], ra[32:48, :]), either(px, ra[32:48, :], rb[32:48, :])
     full = side[...] + jnp.concatenate([low, high], axis=1)
     send_a[...] = full[0:8]
     send_b[...] = full[8:16]
 
 
-def finish_kernel(core, xa, xb, ya, yb, s, ac, out):
+def finish_kernel(core, s, ac, xa, xb, ya, yb, out):
     px, py = parity("gx"), parity("gy")
     low, high = either(px, xb[0:32, :], xa[0:32, :]), either(px, xa[0:32, :], xb[0:32, :])
     left, right = either(py, yb[...], ya[...]), either(py, ya[...], yb[...])
@@ -479,7 +479,7 @@
         name="pack_y",
         limit=8 * 2**20,
     )(st, ld, active)
-    ya, yb = exchange(ya, yb, "gy")
+    ys = exchange(ya, yb, "gy")
     sq = ((256, 256), bf16)
     *mats, inv0, listed = call(
         build_kernel,
@@ -506,63 +506,46 @@
     sw, lw, aw, xa, xb = call(
         pack_x_kernel,
         [((256, 256), f32), ((256, 256), f32), ((32, 256), f32), ((120, 128), f32), ((120, 128), f32)],
-        [VMEM] * 6,
+        [VMEM] * (4 + len(ys)),
         name="pack_x",
-    )(lh, s, l, ac, ya, yb)
+    )(lh, s, l, ac, *ys)
     inner_outs = [
         ((256, 512), bf16), ((256, 512), bf16),
         ((320, 256), bf16), ((320, 256), bf16), ((192, 256), bf16), ((192, 256), bf16),
         ((192, 256), f32), ((PATCH, 256, 256), bf16),
     ]
     inner_args = (sw, lw, aw, yh, yl, lh, ll, ayh, ayl, khl, kth, ktl, dinv, listed, inverse)
-    *early, xb = call(
-        inner_early_kernel,
-        inner_outs + [((120, 128), f32)],
-        [VMEM] * 14 + [ANY, VMEM],
-        [dma],
-        name="inner_early",
-    )(*inner_args, xb)
-    xa, xb = exchange(xa, xb, "gx")
+    xs = exchange(xa, xb, "gx")
     syh, syl, rh, rl, ryh, ryl, tin, inv1 = call(
-        inner_kernel,
-        inner_outs,
-        [VMEM] * 14 + [ANY] + [VMEM] * 8,
-        [dma],
-        name="inner",
-        aliases={15 + n: n for n in range(8)},
-    )(*inner_args, *early)
+        inner_kernel, inner_outs, [VMEM] * 14 + [ANY], [dma], name="inner"
+    )(*inner_args)
     first, last, cut, xa, xb = call(
         edge_kernel,
         [
             ((96, 256), f32), ((96, 256), f32), ((320, 256), f32),
             ((48, 128), f32), ((48, 128), f32),
         ],
-        [ANY] + [VMEM] * 31,
-        [
-            pltpu.VMEM((320, 256), bf16),
-            pltpu.VMEM((320, 256), bf16),
-            pltpu.SMEM((2,), jnp.int32),
-            dma,
-        ],
+        [VMEM] * (29 + len(xs)),
+        [pltpu.VMEM((320, 256), bf16), pltpu.VMEM((320, 256), bf16)],
         name="edge",
     )(
-        cols_in, lw, aw, xa, xb, syh, syl, rh, rl, ryh, ryl, inv0, inv1, listed,
-        yh, yl, lh, ll, ayh, ayl, ath, atl, khl, kth, ktl, dinv, *cutters,
-    )
-    xa, xb = exchange(xa, xb, "gx")
+        lw, aw, syh, syl, rh, rl, ryh, ryl, inv0, inv1, listed,
+        yh, yl, lh, ll, ayh, ayl, ath, atl, khl, kth, ktl, dinv, *cutters, *xs,
+    )
+    xs = exchange(xa, xb, "gx")
     core, side = call(
         spread_kernel,
         [((256, 128), f32), ((16, 256), f32)],
-        [ANY] + [VMEM] * 16,
-        [pltpu.VMEM((320, 256), f32), pltpu.SMEM((2,), jnp.int32), dma],
+        [VMEM] * 17,
+        [pltpu.VMEM((320, 256), f32)],
         name="spread",
-    )(cols_in, first, last, tin, cut, ath, atl, rh, rl, inv0, inv1, *cutters)
+    )(listed, first, last, tin, cut, ath, atl, rh, rl, inv0, inv1, *cutters)
     ya, yb = call(
-        join_x_kernel, [((8, 256), f32), ((8, 256), f32)], [VMEM] * 3, name="join_x"
-    )(side, xa, xb)
-    ya, yb = exchange(ya, yb, "gy")
+        join_x_kernel, [((8, 256), f32), ((8, 256), f32)], [VMEM] * (1 + len(xs)), name="join_x"
+    )(side, *xs)
+    ys = exchange(ya, yb, "gy")
     (out,) = call(finish_kernel, [((256, 128), f32)], [VMEM] * 7, name="finish")(
-        core, xa, xb, ya, yb, s, ac
+        core, s, ac, *xs, *ys
     )
     return out.reshape(8, 32, 128)
 

time: 42.2 us -> 40.3 us (0.955); the launches traced: 41.9 us -> 40.5 us
  waiting for transfers between devices: 9.84 us -> 6.83 us
  starting transfers between devices: 22.5 us -> 23.8 us
    ppermute x4, waiting for transfers between devices: 9.83 us -> 6.82 us  [exchange(): lax.ppermute(b, axis, swaps(axis, 1))]
    ppermute x4, starting transfers between devices: 20.3 us -> 21.6 us  [exchange(): lax.ppermute(b, axis, swaps(axis, 1))]
    pallas_call x1, Pallas kernels: 1.76 us -> 2.52 us  [on_device(): call(edge_kernel, [((96, 256), f32), ((96, 256), f32), ((320, 256), f32),...]
    pallas_call x4 -> x3, Pallas kernels: 2.91 us -> 2.56 us  [the longest x1 2.2 us: on_device(): call(inner_kernel, inner_outs, [VMEM] * 14 + [ANY], [dma], name='inner')]
  transfers between devices with their start and end apart: 8 -> 8, of which waited for: 3 -> 3; matrix products, arithmetic and copies ran while one was open for 0% -> 0% of each run, Pallas kernels for 13% -> 12%
where the time goes in v4:
time: 40.3 us; the launch traced here: 40.5 us
  starting transfers between devices  23.8 us (59%)
  Pallas kernels  9.78 us (24%)
  waiting for transfers between devices  6.83 us (17%)
    ppermute x4, starting transfers between devices, exchange(): lax.ppermute(b, axis, swaps(axis, 1))  21.6 us
    ppermute x4, waiting for transfers between devices, exchange(): lax.ppermute(b, axis, swaps(axis, 1))  6.82 us
    pallas_call x1, Pallas kernels, on_device(): call(edge_kernel, [((96, 256), f32), ((96, 256), f32), ((320, 256), f32),...  2.52 us
    pallas_call x1, Pallas kernels, on_device(): call(build_kernel, [((256, 512), bf16), ((256, 512), bf16), ((64, 256), b...  2.49 us
    pallas_call x1, Pallas kernels, on_device(): call(inner_kernel, inner_outs, [VMEM] * 14 + [ANY], [dma], name='inner')  2.2 us
    ppermute x4, starting transfers between devices, exchange(): lax.ppermute(a, axis, swaps(axis, 0))  2.15 us
    pallas_call x1, Pallas kernels, on_device(): call(pack_y_kernel, [((256, 128), f32), ((256, 128), f32), ((32, 128), f3...  1.2 us
    pallas_call x1, Pallas kernels, on_device(): call(finish_kernel, [((256, 128), f32)], [VMEM] * 7, name='finish')  0.83 us
  transfers between devices with their start and end apart: 8, of which 3 were waited for; matrix products, arithmetic and copies ran while one was open for 0% of the time, Pallas kernels for 12%

profile of v4, /device:TPU:24, one launch (start us, length us, event | category | flops | bytes accessed | tf_op | source)
XLA Modules:
  0.0 40.5 jit_solution(6047629844484001659)
XLA Ops:
  0.0 1.2 %pack_y.1 = (f32[256,128]{1,0:T(8,128)S(1)}, f32[256,128]{1,0:T(8,128)S(1)}, f32[32,128]{1,0:T(8,128)S(1)}, f32[8,640]{1,0:T(8,128)S(1)}, f32[8,640]{1,0:T(8,128)S(1)}) custom-call(f32[256,128]{1,0:T(8,128)} %bitcast.7, bf16[256,128]{1,0:T(8,128)(2,1)} %bitcast.8, s32[32,128]{1,0:T(8,128)} %ac_hbm.1), custom_call_target="tpu_custom_call" | custom-call | flops 1000000 | bytes 1000000 | tf_op jit(solution)/shard_map/pack_y/pallas_call | solution.py:468
  1.2 0.1 collective-permute-start
  1.3 4.9 %collective-permute-start.1 = (f32[8,640]{1,0:T(8,128)S(1)}, f32[8,640]{1,0:T(8,128)S(1)}, u32[]{:S(2)}, u32[]{:S(2)}) collective-permute-start(f32[8,640]{1,0:T(8,128)S(1)} %get-tuple-element.58), channel_id=1, source_target_pairs={{1,2},{3,4},{5,6},{7,8},{9,10},{11,12},{13,14},{2,1},{4,3},{6,5},{... | collective-permute-start | bytes 61448 | tf_op jit(solution)/shard_map/ppermute | solution.py:447
  6.2 2.5 %build.1 = (bf16[256,512]{1,0:T(8,128)(2,1)S(1)}, bf16[256,512]{1,0:T(8,128)(2,1)S(1)}, bf16[64,256]{1,0:T(8,128)(2,1)S(1)}, bf16[64,256]{1,0:T(8,128)(2,1)S(1)}...) custom-call(f32[32,128]{1,0:T(8,128)S(1)} %get-tuple-element.52.afte, ...), custom_call_target="tpu_custom_call" | custom-call | flops 1000000 | bytes 1000000 | tf_op jit(solution)/shard_map/build/pallas_call | solution.py:484
  8.7 0.0 collective-permute-done.refs_0_
  8.8 0.0 collective-permute-done.1.refs_1_
  8.8 0.2 pack_x.1
  9.0 2.0 %collective-permute-start.2 = (f32[120,128]{1,0:T(8,128)S(1)}, f32[120,128]{1,0:T(8,128)S(1)}, u32[]{:S(2)}, u32[]{:S(2)}) collective-permute-start(f32[120,128]{1,0:T(8,128)S(1)} %get-tuple-element.87), channel_id=1, source_target_pairs={{0,16},{32,48},{64,80},{96,112},{128,144},{160,176},{192,208},{224... | collective-permute-start | bytes 184328 | tf_op jit(solution)/shard_map/ppermute | solution.py:447
  10.9 7.3 %collective-permute-start.3 = (f32[120,128]{1,0:T(8,128)S(1)}, f32[120,128]{1,0:T(8,128)S(1)}, u32[]{:S(2)}, u32[]{:S(2)}) collective-permute-start(f32[120,128]{1,0:T(8,128)S(1)} %get-tuple-element.88), channel_id=1, source_target_pairs={{16,32},{48,64},{80,96},{112,128},{144,160},{176,192},{208,224},{3... | collective-permute-start | bytes 184328 | tf_op jit(solution)/shard_map/ppermute | solution.py:447
  18.2 2.2 %inner.1 = (bf16[256,512]{1,0:T(8,128)(2,1)S(1)}, bf16[256,512]{1,0:T(8,128)(2,1)S(1)}, bf16[320,256]{1,0:T(8,128)(2,1)S(1)}, bf16[320,256]{1,0:T(8,128)(2,1)S(1...) custom-call(f32[256,256]{1,0:T(8,128)S(1)} %get-tuple-element.61.sw,, ...), custom_call_target="tpu_custom_call" | custom-call | flops 1000000 | bytes 1000000 | tf_op jit(solution)/shard_map/inner/pallas_call | solution.py:519
  20.4 0.0 collective-permute-done.2.refs_0_
  20.4 0.2 collective-permute-done.3.refs_1_
  20.6 2.5 %edge.1 = (f32[96,256]{1,0:T(8,128)S(1)}, f32[96,256]{1,0:T(8,128)S(1)}, f32[320,256]{1,0:T(8,128)S(1)}, f32[48,128]{1,0:T(8,128)S(1)}, f32[48,128]{1,0:T(8,128)S(1)}) custom-call(f32[256,256]{1,0:T(8,128)S(1)} %get-tuple-element.59.lw, f32[32,256]{1,0:T(8,128)S(1)} %get-tuple-element.60.aw, bf16[256,512]{1,0:T(8,128)(2,1)S(1)} %get-tuple-element.71.syh, ...), custom_call_target="tpu_custom_call" | custom-call | flops 1000000 | bytes 1000000 | tf_op jit(solution)/shard_map/edge/pallas_call | solution.py:522
  23.2 0.1 collective-permute-start.4
  23.2 7.3 %collective-permute-start.5 = (f32[48,128]{1,0:T(8,128)S(1)}, f32[48,128]{1,0:T(8,128)S(1)}, u32[]{:S(2)}, u32[]{:S(2)}) collective-permute-start(f32[48,128]{1,0:T(8,128)S(1)} %get-tuple-element.95), channel_id=1, source_target_pairs={{16,32},{48,64},{80,96},{112,128},{144,160},{176,192},{208,224},{3... | collective-permute-start | bytes 73736 | tf_op jit(solution)/shard_map/ppermute | solution.py:447
  30.5 0.4 spread.1
  30.9 0.0 collective-permute-done.4.refs_0_.xa
  30.9 1.7 %collective-permute-done.5.refs_1_.xb = f32[48,128]{1,0:T(8,128)S(1)} collective-permute-done((f32[48,128]{1,0:T(8,128)S(1)}, f32[48,128]{1,0:T(8,128)S(1)}, u32[]{:S(2)}, u32[]{:S(2)}) %collective-permute-start.5) | collective-permute-done | bytes 24608 | tf_op jit(solution)/shard_map/ppermute | solution.py:447
  32.6 0.0 collective-permute-start.6
  32.6 2.2 %collective-permute-start.7 = (f32[8,256]{1,0:T(8,128)S(1)}, f32[8,256]{1,0:T(8,128)S(1)}, u32[]{:S(2)}, u32[]{:S(2)}) collective-permute-start(f32[8,256]{1,0:T(8,128)S(1)} %get-tuple-element.98), channel_id=1, source_target_pairs={{1,2},{3,4},{5,6},{7,8},{9,10},{11,12},{13,14},{2,1},{4,3},{6,5},{... | collective-permute-start | bytes 24584 | tf_op jit(solution)/shard_map/ppermute | solution.py:447
  34.8 0.0 collective-permute-done.6.ya
  34.8 4.9 %collective-permute-done.7.yb = f32[8,256]{1,0:T(8,128)S(1)} collective-permute-done((f32[8,256]{1,0:T(8,128)S(1)}, f32[8,256]{1,0:T(8,128)S(1)}, u32[]{:S(2)}, u32[]{:S(2)}) %collective-permute-start.7) | collective-permute-done | bytes 8224 | tf_op jit(solution)/shard_map/ppermute | solution.py:447
  39.7 0.8 %finish.1 = f32[256,128]{1,0:T(8,128)} custom-call(f32[256,128]{1,0:T(8,128)S(1)} %get-tuple-element.93.core, f32[256,128]{1,0:T(8,128)S(1)} %get-tuple-element.55.s, f32[32,128]{1,0:T(8,128)S(1)} %get-tuple-element.52.after.ac, f32[48,128]{1,0:T(8,128)S(1)} %collective-permute-done.4.refs_0_.xa, f32[48,128]{1,0:T(8,128)S(1)} %collective-permute-done.5.refs_1_.xb, ...), custom_call_target="tpu_custom_call" | custom-call | flops 1000000 | bytes 1000000 | tf_op jit(solution)/shard_map/finish/pallas_call | solution.py:547
  (1 shorter events, 0.0 us)
Async XLA Ops:
  1.2 7.5 %collective-permute-start = (f32[8,640]{1,0:T(8,128)S(1)}, f32[8,640]{1,0:T(8,128)S(1)}, u32[]{:S(2)}, u32[]{:S(2)}) collective-permute-start(f32[8,640]{1,0:T(8,128)S(1)} %get-tuple-element.57), channel_id=1, source_target_pairs={{0,1},{2,3},{4,5},{6,7},{8,9},{10,11},{12,13},{14,15},{1,0},{3,2},... | collective-permute-start | bytes 61448 | tf_op jit(solution)/shard_map/ppermute | solution.py:447
  1.3 7.5 %collective-permute-start.1 = (f32[8,640]{1,0:T(8,128)S(1)}, f32[8,640]{1,0:T(8,128)S(1)}, u32[]{:S(2)}, u32[]{:S(2)}) collective-permute-start(f32[8,640]{1,0:T(8,128)S(1)} %get-tuple-element.58), channel_id=1, source_target_pairs={{1,2},{3,4},{5,6},{7,8},{9,10},{11,12},{13,14},{2,1},{4,3},{6,5},{... | collective-permute-start | bytes 61448 | tf_op jit(solution)/shard_map/ppermute | solution.py:447
  9.0 11.5 %collective-permute-start.2 = (f32[120,128]{1,0:T(8,128)S(1)}, f32[120,128]{1,0:T(8,128)S(1)}, u32[]{:S(2)}, u32[]{:S(2)}) collective-permute-start(f32[120,128]{1,0:T(8,128)S(1)} %get-tuple-element.87), channel_id=1, source_target_pairs={{0,16},{32,48},{64,80},{96,112},{128,144},{160,176},{192,208},{224... | collective-permute-start | bytes 184328 | tf_op jit(solution)/shard_map/ppermute | solution.py:447
  10.9 9.7 %collective-permute-start.3 = (f32[120,128]{1,0:T(8,128)S(1)}, f32[120,128]{1,0:T(8,128)S(1)}, u32[]{:S(2)}, u32[]{:S(2)}) collective-permute-start(f32[120,128]{1,0:T(8,128)S(1)} %get-tuple-element.88), channel_id=1, source_target_pairs={{16,32},{48,64},{80,96},{112,128},{144,160},{176,192},{208,224},{3... | collective-permute-start | bytes 184328 | tf_op jit(solution)/shard_map/ppermute | solution.py:447
  23.2 7.7 %collective-permute-start.4 = (f32[48,128]{1,0:T(8,128)S(1)}, f32[48,128]{1,0:T(8,128)S(1)}, u32[]{:S(2)}, u32[]{:S(2)}) collective-permute-start(f32[48,128]{1,0:T(8,128)S(1)} %get-tuple-element.94), channel_id=1, source_target_pairs={{0,16},{32,48},{64,80},{96,112},{128,144},{160,176},{192,208},{224... | collective-permute-start | bytes 73736 | tf_op jit(solution)/shard_map/ppermute | solution.py:447
  23.2 9.3 %collective-permute-start.5 = (f32[48,128]{1,0:T(8,128)S(1)}, f32[48,128]{1,0:T(8,128)S(1)}, u32[]{:S(2)}, u32[]{:S(2)}) collective-permute-start(f32[48,128]{1,0:T(8,128)S(1)} %get-tuple-element.95), channel_id=1, source_target_pairs={{16,32},{48,64},{80,96},{112,128},{144,160},{176,192},{208,224},{3... | collective-permute-start | bytes 73736 | tf_op jit(solution)/shard_map/ppermute | solution.py:447
  32.6 2.2 %collective-permute-start.6 = (f32[8,256]{1,0:T(8,128)S(1)}, f32[8,256]{1,0:T(8,128)S(1)}, u32[]{:S(2)}, u32[]{:S(2)}) collective-permute-start(f32[8,256]{1,0:T(8,128)S(1)} %get-tuple-element.97), channel_id=1, source_target_pairs={{0,1},{2,3},{4,5},{6,7},{8,9},{10,11},{12,13},{14,15},{1,0},{3,2},... | collective-permute-start | bytes 24584 | tf_op jit(solution)/shard_map/ppermute | solution.py:447
  32.6 7.1 %collective-permute-start.7 = (f32[8,256]{1,0:T(8,128)S(1)}, f32[8,256]{1,0:T(8,128)S(1)}, u32[]{:S(2)}, u32[]{:S(2)}) collective-permute-start(f32[8,256]{1,0:T(8,128)S(1)} %get-tuple-element.98), channel_id=1, source_target_pairs={{1,2},{3,4},{5,6},{7,8},{9,10},{11,12},{13,14},{2,1},{4,3},{6,5},{... | collective-permute-start | bytes 24584 | tf_op jit(solution)/shard_map/ppermute | solution.py:447

commit v5 on v4

--- a/solution.py
+++ b/solution.py
@@ -75,23 +75,20 @@
     return out
 
 
-def fetch(pairs, sem):
+def either(flag, a, b):
+    return jnp.where(flag == 0, a, b)
+
+
+def pack_y_kernel(
+    st_hbm, ld_hbm, ac_hbm, s_out, l_out, a_out, send_a, send_b, st, ld, ac, wide, sem
+):
+    pairs = [(st_hbm, st), (ld_hbm, ld), (ac_hbm, ac)]
     copies = [pltpu.make_async_copy(a, b, sem.at[n]) for n, (a, b) in enumerate(pairs)]
     for copy in copies:
         copy.start()
+    py = parity("gy")
     for copy in copies:
         copy.wait()
-
-
-def either(flag, a, b):
-    return jnp.where(flag == 0, a, b)
-
-
-def pack_y_kernel(
-    st_hbm, ld_hbm, ac_hbm, s_out, l_out, a_out, send_a, send_b, st, ld, ac, wide, sem
-):
-    fetch([(st_hbm, st), (ld_hbm, ld), (ac_hbm, ac)], sem)
-    py = parity("gy")
     wide[...] = ld[...].astype(f32)
     for x in range(32):
         s_out[8 * x : 8 * x + 8, :] = st[pl.ds(x, 8, stride=32), :]
@@ -181,7 +178,7 @@
     for m in range(2):
         a = cols[m] >> 4
         need.append((a == places[0]) | (a == places[1]))
-    for ms in ((), (0,), (1,), (0, 1)):
+    for ms in ((0, 1), (1,), (0,), ()):
         wanted = [need[m] if m in ms else jnp.logical_not(need[m]) for m in range(2)]
         pl.when(wanted[0] & wanted[1])(lambda ms=ms: body(ms))
 
@@ -356,18 +353,19 @@
     stiff, mass, basis, values, cols, sem,
 ):
     del after
+    pairs = [
+        (stiff_hbm, stiff),
+        (mass_hbm, mass),
+        (basis_hbm, basis),
+        (values_hbm, values),
+        (cols_hbm, cols),
+    ]
+    small = [pltpu.make_async_copy(a, b, sem.at[n]) for n, (a, b) in enumerate(pairs)]
     bulk = pltpu.make_async_copy(inverse.at[0], inv, sem.at[5])
-    bulk.start()
-    fetch(
-        [
-            (stiff_hbm, stiff),
-            (mass_hbm, mass),
-            (basis_hbm, basis),
-            (values_hbm, values),
-            (cols_hbm, cols),
-        ],
-        sem,
-    )
+    for copy in small + [bulk]:
+        copy.start()
+    for copy in small:
+        copy.wait()
     py = parity("gy")
     kz, kx, ky = ([stiff[d, k] for k in range(BAND + 1)] for d in range(3))
     mz, mx, my = ([mass[d, k] for k in range(BAND + 1)] for d in range(3))

time: 40.3 us -> 40.5 us (level)
  waiting for transfers between devices: 6.83 us -> 4.31 us
  starting transfers between devices: 23.8 us -> 25.6 us
  Pallas kernels: 9.78 us -> 10.3 us
    ppermute x4, waiting for transfers between devices: 6.82 us -> 4.3 us  [exchange(): lax.ppermute(b, axis, swaps(axis, 1))]
    ppermute x4, starting transfers between devices: 21.6 us -> 23.4 us  [exchange(): lax.ppermute(b, axis, swaps(axis, 1))]
    pallas_call x1, Pallas kernels: 0.36 us -> 1.41 us  [on_device(): call(spread_kernel, [((256, 128), f32), ((16, 256), f32)], [VMEM] * 17, [...]
    pallas_call x1, Pallas kernels: 2.49 us -> 1.96 us  [on_device(): call(build_kernel, [((256, 512), bf16), ((256, 512), bf16), ((64, 256), b...]
  transfers between devices with their start and end apart: 8 -> 8, of which waited for: 3 -> 3; matrix products, arithmetic and copies ran while one was open for 0% -> 0% of each run, Pallas kernels for 12% -> 14%
where the time goes in v5:
time: 40.5 us; the launch traced here: 40.3 us
  starting transfers between devices  25.6 us (63%)
  Pallas kernels  10.3 us (25%)
  waiting for transfers between devices  4.31 us (11%)
    ppermute x4, starting transfers between devices, exchange(): lax.ppermute(b, axis, swaps(axis, 1))  23.4 us
    ppermute x4, waiting for transfers between devices, exchange(): lax.ppermute(b, axis, swaps(axis, 1))  4.3 us
    pallas_call x1, Pallas kernels, on_device(): call(edge_kernel, [((96, 256), f32), ((96, 256), f32), ((320, 256), f32),...  2.53 us
    pallas_call x1, Pallas kernels, on_device(): call(inner_kernel, inner_outs, [VMEM] * 14 + [ANY], [dma], name='inner')  2.2 us
    ppermute x4, starting transfers between devices, exchange(): lax.ppermute(a, axis, swaps(axis, 0))  2.15 us
    pallas_call x1, Pallas kernels, on_device(): call(build_kernel, [((256, 512), bf16), ((256, 512), bf16), ((64, 256), b...  1.96 us
    pallas_call x1, Pallas kernels, on_device(): call(spread_kernel, [((256, 128), f32), ((16, 256), f32)], [VMEM] * 17, [...  1.41 us
    pallas_call x1, Pallas kernels, on_device(): call(pack_y_kernel, [((256, 128), f32), ((256, 128), f32), ((32, 128), f3...  1.2 us
  transfers between devices with their start and end apart: 8, of which 3 were waited for; matrix products, arithmetic and copies ran while one was open for 0% of the time, Pallas kernels for 14%

profile of v5, /device:TPU:24, one launch (start us, length us, event | category | flops | bytes accessed | tf_op | source)
XLA Modules:
  0.0 40.3 jit_solution(689847281702977869)
XLA Ops:
  0.0 1.2 %pack_y.1 = (f32[256,128]{1,0:T(8,128)S(1)}, f32[256,128]{1,0:T(8,128)S(1)}, f32[32,128]{1,0:T(8,128)S(1)}, f32[8,640]{1,0:T(8,128)S(1)}, f32[8,640]{1,0:T(8,128)S(1)}) custom-call(f32[256,128]{1,0:T(8,128)} %bitcast.7, bf16[256,128]{1,0:T(8,128)(2,1)} %bitcast.8, s32[32,128]{1,0:T(8,128)} %ac_hbm.1), custom_call_target="tpu_custom_call" | custom-call | flops 1000000 | bytes 1000000 | tf_op jit(solution)/shard_map/pack_y/pallas_call | solution.py:466
  1.2 0.1 collective-permute-start
  1.3 4.9 %collective-permute-start.1 = (f32[8,640]{1,0:T(8,128)S(1)}, f32[8,640]{1,0:T(8,128)S(1)}, u32[]{:S(2)}, u32[]{:S(2)}) collective-permute-start(f32[8,640]{1,0:T(8,128)S(1)} %get-tuple-element.58), channel_id=1, source_target_pairs={{1,2},{3,4},{5,6},{7,8},{9,10},{11,12},{13,14},{2,1},{4,3},{6,5},{... | collective-permute-start | bytes 61448 | tf_op jit(solution)/shard_map/ppermute | solution.py:445
  6.2 2.0 %build.1 = (bf16[256,512]{1,0:T(8,128)(2,1)S(1)}, bf16[256,512]{1,0:T(8,128)(2,1)S(1)}, bf16[64,256]{1,0:T(8,128)(2,1)S(1)}, bf16[64,256]{1,0:T(8,128)(2,1)S(1)}...) custom-call(f32[32,128]{1,0:T(8,128)S(1)} %get-tuple-element.52.afte, ...), custom_call_target="tpu_custom_call" | custom-call | flops 1000000 | bytes 1000000 | tf_op jit(solution)/shard_map/build/pallas_call | solution.py:482
  8.2 0.0 collective-permute-done.refs_0_
  8.2 0.3 collective-permute-done.1.refs_1_
  8.5 0.2 pack_x.1
  8.7 2.0 %collective-permute-start.2 = (f32[120,128]{1,0:T(8,128)S(1)}, f32[120,128]{1,0:T(8,128)S(1)}, u32[]{:S(2)}, u32[]{:S(2)}) collective-permute-start(f32[120,128]{1,0:T(8,128)S(1)} %get-tuple-element.87), channel_id=1, source_target_pairs={{0,16},{32,48},{64,80},{96,112},{128,144},{160,176},{192,208},{224... | collective-permute-start | bytes 184328 | tf_op jit(solution)/shard_map/ppermute | solution.py:445
  10.7 7.5 %collective-permute-start.3 = (f32[120,128]{1,0:T(8,128)S(1)}, f32[120,128]{1,0:T(8,128)S(1)}, u32[]{:S(2)}, u32[]{:S(2)}) collective-permute-start(f32[120,128]{1,0:T(8,128)S(1)} %get-tuple-element.88), channel_id=1, source_target_pairs={{16,32},{48,64},{80,96},{112,128},{144,160},{176,192},{208,224},{3... | collective-permute-start | bytes 184328 | tf_op jit(solution)/shard_map/ppermute | solution.py:445
  18.2 2.2 %inner.1 = (bf16[256,512]{1,0:T(8,128)(2,1)S(1)}, bf16[256,512]{1,0:T(8,128)(2,1)S(1)}, bf16[320,256]{1,0:T(8,128)(2,1)S(1)}, bf16[320,256]{1,0:T(8,128)(2,1)S(1...) custom-call(f32[256,256]{1,0:T(8,128)S(1)} %get-tuple-element.61.sw,, ...), custom_call_target="tpu_custom_call" | custom-call | flops 1000000 | bytes 1000000 | tf_op jit(solution)/shard_map/inner/pallas_call | solution.py:517
  20.4 0.0 collective-permute-done.2.refs_0_
  20.4 0.0 collective-permute-done.3.refs_1_
  20.4 2.5 %edge.1 = (f32[96,256]{1,0:T(8,128)S(1)}, f32[96,256]{1,0:T(8,128)S(1)}, f32[320,256]{1,0:T(8,128)S(1)}, f32[48,128]{1,0:T(8,128)S(1)}, f32[48,128]{1,0:T(8,128)S(1)}) custom-call(f32[256,256]{1,0:T(8,128)S(1)} %get-tuple-element.59.lw, f32[32,256]{1,0:T(8,128)S(1)} %get-tuple-element.60.aw, bf16[256,512]{1,0:T(8,128)(2,1)S(1)} %get-tuple-element.71.syh, ...), custom_call_target="tpu_custom_call" | custom-call | flops 1000000 | bytes 1000000 | tf_op jit(solution)/shard_map/edge/pallas_call | solution.py:520
  23.0 0.1 collective-permute-start.4
  23.0 7.5 %collective-permute-start.5 = (f32[48,128]{1,0:T(8,128)S(1)}, f32[48,128]{1,0:T(8,128)S(1)}, u32[]{:S(2)}, u32[]{:S(2)}) collective-permute-start(f32[48,128]{1,0:T(8,128)S(1)} %get-tuple-element.95), channel_id=1, source_target_pairs={{16,32},{48,64},{80,96},{112,128},{144,160},{176,192},{208,224},{3... | collective-permute-start | bytes 73736 | tf_op jit(solution)/shard_map/ppermute | solution.py:445
  30.5 1.4 %spread.1 = (f32[256,128]{1,0:T(8,128)S(1)}, f32[16,256]{1,0:T(8,128)S(1)}) custom-call(s32[16,128]{1,0:T(8,128)S(1)} %get-tuple-element.53.listed, f32[96,256]{1,0:T(8,128)S(1)} %get-tuple-element.89.first, f32[96,256]{1,0:T(8,128)S(1)} %get-tuple-element.90.last, f32[192,256]{1,0:T(8,128)S(1)} %get-tuple-element.91.tin, ...), custom_call_target="tpu_custom_call" | custom-call | flops 1000000 | bytes 1000000 | tf_op jit(solution)/shard_map/spread/pallas_call | solution.py:534
  31.9 0.0 collective-permute-done.4.refs_0_.xa
  31.9 0.5 %collective-permute-done.5.refs_1_.xb = f32[48,128]{1,0:T(8,128)S(1)} collective-permute-done((f32[48,128]{1,0:T(8,128)S(1)}, f32[48,128]{1,0:T(8,128)S(1)}, u32[]{:S(2)}, u32[]{:S(2)}) %collective-permute-start.5) | collective-permute-done | bytes 24608 | tf_op jit(solution)/shard_map/ppermute | solution.py:445
  32.4 0.0 collective-permute-start.6
  32.4 3.5 %collective-permute-start.7 = (f32[8,256]{1,0:T(8,128)S(1)}, f32[8,256]{1,0:T(8,128)S(1)}, u32[]{:S(2)}, u32[]{:S(2)}) collective-permute-start(f32[8,256]{1,0:T(8,128)S(1)} %get-tuple-element.98), channel_id=1, source_target_pairs={{1,2},{3,4},{5,6},{7,8},{9,10},{11,12},{13,14},{2,1},{4,3},{6,5},{... | collective-permute-start | bytes 24584 | tf_op jit(solution)/shard_map/ppermute | solution.py:445
  35.9 0.0 collective-permute-done.6.ya
  35.9 3.5 %collective-permute-done.7.yb = f32[8,256]{1,0:T(8,128)S(1)} collective-permute-done((f32[8,256]{1,0:T(8,128)S(1)}, f32[8,256]{1,0:T(8,128)S(1)}, u32[]{:S(2)}, u32[]{:S(2)}) %collective-permute-start.7) | collective-permute-done | bytes 8224 | tf_op jit(solution)/shard_map/ppermute | solution.py:445
  39.5 0.8 %finish.1 = f32[256,128]{1,0:T(8,128)} custom-call(f32[256,128]{1,0:T(8,128)S(1)} %get-tuple-element.93.core, f32[256,128]{1,0:T(8,128)S(1)} %get-tuple-element.55.s, f32[32,128]{1,0:T(8,128)S(1)} %get-tuple-element.52.after.ac, f32[48,128]{1,0:T(8,128)S(1)} %collective-permute-done.4.refs_0_.xa, f32[48,128]{1,0:T(8,128)S(1)} %collective-permute-done.5.refs_1_.xb, ...), custom_call_target="tpu_custom_call" | custom-call | flops 1000000 | bytes 1000000 | tf_op jit(solution)/shard_map/finish/pallas_call | solution.py:545
  (1 shorter events, 0.0 us)
Async XLA Ops:
  1.2 7.0 %collective-permute-start = (f32[8,640]{1,0:T(8,128)S(1)}, f32[8,640]{1,0:T(8,128)S(1)}, u32[]{:S(2)}, u32[]{:S(2)}) collective-permute-start(f32[8,640]{1,0:T(8,128)S(1)} %get-tuple-element.57), channel_id=1, source_target_pairs={{0,1},{2,3},{4,5},{6,7},{8,9},{10,11},{12,13},{14,15},{1,0},{3,2},... | collective-permute-start | bytes 61448 | tf_op jit(solution)/shard_map/ppermute | solution.py:445
  1.3 7.2 %collective-permute-start.1 = (f32[8,640]{1,0:T(8,128)S(1)}, f32[8,640]{1,0:T(8,128)S(1)}, u32[]{:S(2)}, u32[]{:S(2)}) collective-permute-start(f32[8,640]{1,0:T(8,128)S(1)} %get-tuple-element.58), channel_id=1, source_target_pairs={{1,2},{3,4},{5,6},{7,8},{9,10},{11,12},{13,14},{2,1},{4,3},{6,5},{... | collective-permute-start | bytes 61448 | tf_op jit(solution)/shard_map/ppermute | solution.py:445
  8.7 11.7 %collective-permute-start.2 = (f32[120,128]{1,0:T(8,128)S(1)}, f32[120,128]{1,0:T(8,128)S(1)}, u32[]{:S(2)}, u32[]{:S(2)}) collective-permute-start(f32[120,128]{1,0:T(8,128)S(1)} %get-tuple-element.87), channel_id=1, source_target_pairs={{0,16},{32,48},{64,80},{96,112},{128,144},{160,176},{192,208},{224... | collective-permute-start | bytes 184328 | tf_op jit(solution)/shard_map/ppermute | solution.py:445
  10.7 9.7 %collective-permute-start.3 = (f32[120,128]{1,0:T(8,128)S(1)}, f32[120,128]{1,0:T(8,128)S(1)}, u32[]{:S(2)}, u32[]{:S(2)}) collective-permute-start(f32[120,128]{1,0:T(8,128)S(1)} %get-tuple-element.88), channel_id=1, source_target_pairs={{16,32},{48,64},{80,96},{112,128},{144,160},{176,192},{208,224},{3... | collective-permute-start | bytes 184328 | tf_op jit(solution)/shard_map/ppermute | solution.py:445
  23.0 9.0 %collective-permute-start.4 = (f32[48,128]{1,0:T(8,128)S(1)}, f32[48,128]{1,0:T(8,128)S(1)}, u32[]{:S(2)}, u32[]{:S(2)}) collective-permute-start(f32[48,128]{1,0:T(8,128)S(1)} %get-tuple-element.94), channel_id=1, source_target_pairs={{0,16},{32,48},{64,80},{96,112},{128,144},{160,176},{192,208},{224... | collective-permute-start | bytes 73736 | tf_op jit(solution)/shard_map/ppermute | solution.py:445
  23.0 9.3 %collective-permute-start.5 = (f32[48,128]{1,0:T(8,128)S(1)}, f32[48,128]{1,0:T(8,128)S(1)}, u32[]{:S(2)}, u32[]{:S(2)}) collective-permute-start(f32[48,128]{1,0:T(8,128)S(1)} %get-tuple-element.95), channel_id=1, source_target_pairs={{16,32},{48,64},{80,96},{112,128},{144,160},{176,192},{208,224},{3... | collective-permute-start | bytes 73736 | tf_op jit(solution)/shard_map/ppermute | solution.py:445
  32.4 3.5 %collective-permute-start.6 = (f32[8,256]{1,0:T(8,128)S(1)}, f32[8,256]{1,0:T(8,128)S(1)}, u32[]{:S(2)}, u32[]{:S(2)}) collective-permute-start(f32[8,256]{1,0:T(8,128)S(1)} %get-tuple-element.97), channel_id=1, source_target_pairs={{0,1},{2,3},{4,5},{6,7},{8,9},{10,11},{12,13},{14,15},{1,0},{3,2},... | collective-permute-start | bytes 24584 | tf_op jit(solution)/shard_map/ppermute | solution.py:445
  32.4 7.1 %collective-permute-start.7 = (f32[8,256]{1,0:T(8,128)S(1)}, f32[8,256]{1,0:T(8,128)S(1)}, u32[]{:S(2)}, u32[]{:S(2)}) collective-permute-start(f32[8,256]{1,0:T(8,128)S(1)} %get-tuple-element.98), channel_id=1, source_target_pairs={{1,2},{3,4},{5,6},{7,8},{9,10},{11,12},{13,14},{2,1},{4,3},{6,5},{... | collective-permute-start | bytes 24584 | tf_op jit(solution)/shard_map/ppermute | solution.py:445
